TPU v7x, 32 devices: a whole 2x2x4 slice. The times are simulated.
32 devices in a mesh: dp: 4 (over z), rows: 4 (over y, core), cols: 2 (over x).
Axes of the slice: x: 2, y: 2, z: 4, core: 2. Of those that a mesh axis runs over, the one named last changes fastest.
Arguments:
- hidden_in: bfloat16 [3072, 1536], P(('dp', 'cols'), 'rows'), may hold values from -7 to 7
- attn_gain: float32 [2, 1536], P(None, 'rows'), may hold values from 0.1 to 1.9
- w_qkv: bfloat16 [2, 1536, 2048], P(None, 'rows', 'cols'), may hold values from -0.15625 to 0.15625
- b_qkv: float32 [2, 2048], P(None, 'cols'), may hold values from -2 to 2
- w_out: bfloat16 [2, 1536, 1536], P(None, 'cols', 'rows'), may hold values from -0.3125 to 0.3125
- mlp_gain: float32 [2, 1536], P(None, 'rows'), may hold values from 0.1 to 1.9
- w_gate: bfloat16 [2, 1536, 8960], P(None, 'rows', 'cols'), may hold values from -0.15625 to 0.15625
- w_up: bfloat16 [2, 1536, 8960], P(None, 'rows', 'cols'), may hold values from -0.15625 to 0.15625
- w_down: bfloat16 [2, 8960, 1536], P(None, 'cols', 'rows'), may hold values from -0.0625 to 0.0625
- out_grad: bfloat16 [3072, 1536], P(('dp', 'cols'), 'rows'), may hold values from -6 to 6
Outputs:
- hidden_out: bfloat16 [3072, 1536], P(('dp', 'cols'), 'rows')
- in_grad: float32 [3072, 1536], P(('dp', 'cols'), 'rows')
- attn_gain_grad: float32 [2, 1536], P(None, 'rows')
- w_qkv_grad: float32 [2, 1536, 2048], P(None, 'rows', 'cols')
- b_qkv_grad: float32 [2, 2048], P(None, 'cols')
- w_out_grad: float32 [2, 1536, 1536], P(None, 'cols', 'rows')
- mlp_gain_grad: float32 [2, 1536], P(None, 'rows')
- w_gate_grad: float32 [2, 1536, 8960], P(None, 'rows', 'cols')
- w_up_grad: float32 [2, 1536, 8960], P(None, 'rows', 'cols')
- w_down_grad: float32 [2, 8960, 1536], P(None, 'cols', 'rows')
All inputs are finite; a program needn't handle non-finite values.
Results may differ from a plain program's by a relative error of at most 0.025.
Values may be sent and summed in bfloat16 or wider, within the bound.
No kernel may reach another device: no remote copies, remote signals or barrier semaphores. Data moves between devices by JAX's collectives and lax.ppermute only.
A program may use at most 320 MiB of HBM per device.

v0:
```python
import jax
import jax.numpy as jnp
import numpy as np
from jax import lax
from jax.experimental import pallas as pl
from jax.experimental.pallas import tpu as pltpu
from jax.sharding import Mesh, PartitionSpec as P


D = 1536
HEADS = 12
KV_HEADS = 2
HEAD_DIM = 128
SEQ = 192
LAYERS = 2
GROUP = HEADS // KV_HEADS

eps = 1e-06
theta = 1000000.0
masked = -1e30


DP, RY, RK, CX = "dp", "ry", "rk", "cols"
ROWS = (RY, RK)
PLANE = (RY, CX)

f32 = jnp.float32
bf16 = jnp.bfloat16


def mm(left, right):
    return jnp.dot(left, right, preferred_element_type=f32)


def mm_t(left, right):
    return lax.dot_general(left, right, (((1,), (1,)), ((), ())), preferred_element_type=f32)


def t_mm(left, right):
    return lax.dot_general(left, right, (((0,), (0,)), ((), ())), preferred_element_type=f32)


def swap_core(values):
    return lax.ppermute(values, RK, [(0, 1), (1, 0)])


def swap_x(values):
    return lax.ppermute(values, CX, [(0, 1), (1, 0)])


def swap_y(values):
    return lax.ppermute(values, RY, [(0, 1), (1, 0)])


def swap_diagonal(values):
    return lax.ppermute(values, (RK, CX), [(0, 0), (1, 2), (2, 1), (3, 3)])


def gather_eight(values):
    half = values.shape[0] // 2
    by_x = swap_x(values)
    by_y = swap_y(values)
    first = swap_x(by_y[:half])
    second = swap_y(by_x[half:])
    near = jnp.concatenate([values, by_x, by_y, first, second], axis=0)
    return jnp.concatenate([near, swap_core(near)], axis=0)


def scatter_eight(partial):
    rows = partial.shape[0] // 8
    half = rows // 2
    other = swap_core(partial[4 * rows :].astype(bf16))
    summed = partial[: 4 * rows] + other.astype(f32)
    own, to_x, to_y, corner = (summed[i * rows : (i + 1) * rows] for i in range(4))
    corner = corner.astype(bf16)
    via_x = swap_x(corner[:half]).astype(f32)
    via_y = swap_y(corner[half:]).astype(f32)
    to_y = jnp.concatenate([to_y[:half] + via_x, to_y[half:]], axis=0).astype(bf16)
    to_x = jnp.concatenate([to_x[:half], to_x[half:] + via_y], axis=0).astype(bf16)
    from_x = swap_x(to_x).astype(f32)
    return own + from_x + swap_y(to_y).astype(f32)


def rope_tables():
    frequency = theta ** (-np.arange(0, HEAD_DIM, 2, dtype=np.float32) / np.float32(HEAD_DIM))
    angles = np.arange(SEQ, dtype=np.float32)[:, None] * frequency[None, :].astype(np.float32)
    angles = np.concatenate([angles, angles], axis=-1).astype(np.float32)
    return np.cos(angles).astype(np.float32), np.sin(angles).astype(np.float32)


def rotate_half(values):
    half_dim = values.shape[-1] // 2
    return jnp.concatenate([-values[..., half_dim:], values[..., :half_dim]], axis=-1)


def attention_frame():
    second = lax.axis_index(RK) == 1
    cosine, sine = rope_tables()
    half = SEQ // 2
    cosine = jnp.where(second, np.roll(cosine, -half, axis=0), cosine)
    sine = jnp.where(second, np.roll(sine, -half, axis=0), sine)
    position = (jnp.arange(SEQ) + half * lax.axis_index(RK)) % SEQ
    mask = position[:, None] >= position[None, :]
    return cosine, sine, mask


def causal_scores(query_round, key_round, mask):
    raw_scores = jnp.einsum("igd,jd->gij", query_round, key_round, preferred_element_type=f32)
    return jnp.where(mask[None], raw_scores * HEAD_DIM ** (-0.5), masked)


def attention_forward(qkv_rows, frame):
    cosine, sine, mask = frame
    blocks = qkv_rows.reshape(SEQ, GROUP + 2, HEAD_DIM)
    turned = blocks[:, : GROUP + 1]
    turned = turned * cosine[:, None, :] + rotate_half(turned) * sine[:, None, :]
    turned = turned.astype(bf16)
    query_round = turned[:, :GROUP]
    key_round = turned[:, GROUP]
    value_round = blocks[:, GROUP + 1].astype(bf16)
    scores = causal_scores(query_round, key_round, mask)
    highest = jnp.max(scores, axis=-1, keepdims=True)
    log_total = highest + jnp.log(jnp.sum(jnp.exp(scores - highest), axis=-1, keepdims=True))
    weights_round = jnp.exp(scores - log_total).astype(bf16)
    attended = jnp.einsum("gij,jd->igd", weights_round, value_round, preferred_element_type=f32)
    attended = attended.astype(bf16).reshape(SEQ, -1)
    return attended, (query_round, key_round, value_round, log_total)


def attention_backward(grad_attended, kept, frame):
    cosine, sine, mask = frame
    query_round, key_round, value_round, log_total = kept
    grad_round = grad_attended.astype(bf16).reshape(SEQ, GROUP, HEAD_DIM)
    scores = causal_scores(query_round, key_round, mask)
    prob = jnp.exp(scores - log_total)
    weights_round = prob.astype(bf16)
    grad_value = jnp.einsum("gij,igd->jd", weights_round, grad_round, preferred_element_type=f32)
    grad_prob = jnp.einsum("igd,jd->gij", grad_round, value_round, preferred_element_type=f32)
    inner = jnp.sum(prob * grad_prob, axis=-1, keepdims=True)
    grad_scores = (prob * (grad_prob - inner) * HEAD_DIM ** (-0.5)).astype(bf16)
    grad_query = jnp.einsum("gij,jd->igd", grad_scores, key_round, preferred_element_type=f32)
    grad_key = jnp.einsum("gij,igd->jd", grad_scores, query_round, preferred_element_type=f32)
    turned = jnp.concatenate([grad_query, grad_key[:, None]], axis=1)
    turned = turned * cosine[:, None, :] - rotate_half(turned) * sine[:, None, :]
    joined = jnp.concatenate([turned, grad_value[:, None]], axis=1)
    return joined.reshape(SEQ, -1)


def norm_forward(resid, gain_row):
    scale_row = lax.rsqrt(jnp.mean(resid * resid, axis=1) + eps)
    normed = (resid * scale_row[:, None] * gain_row[None, :]).astype(bf16)
    return normed, scale_row


def norm_backward(grad_normed, resid, scale_row, gain_row):
    scaled = grad_normed * gain_row[None, :]
    inner = jnp.sum(scaled * resid, axis=1)
    gain_grad = jnp.sum(grad_normed * resid * scale_row[:, None], axis=0)
    grad_resid = (
        scale_row[:, None] * scaled
        - resid * (scale_row * scale_row * scale_row * inner / D)[:, None]
    )
    return grad_resid, gain_grad


def sum_dp(values):
    if lax.axis_size(DP) != 4:
        summed = lax.psum_scatter(values, DP, scatter_dimension=0, tiled=True)
        return lax.all_gather(summed, DP, axis=0, tiled=True)
    place = lax.axis_index(DP)
    inner = (place == 1) | (place == 2)
    kind = values.dtype
    inward = lax.ppermute(values, DP, [(0, 1), (3, 2)])
    half = (values.astype(f32) + inward.astype(f32)).astype(kind)
    across = lax.ppermute(half, DP, [(1, 2), (2, 1)])
    whole = (half.astype(f32) + across.astype(f32)).astype(kind)
    outward = lax.ppermute(whole, DP, [(1, 0), (2, 3)])
    return jnp.where(inner, whole, outward)


def gather_line(values):
    at = lax.axis_index(DP)
    inner = (at == 1) | (at == 2)
    pair = lax.ppermute(values, DP, [(0, 1), (1, 0), (2, 3), (3, 2)])
    middle = lax.ppermute(values, DP, [(1, 2), (2, 1)])
    outward = lax.ppermute(middle, DP, [(1, 0), (2, 3)])
    across = lax.ppermute(pair, DP, [(1, 2), (2, 1)])
    last = lax.ppermute(across, DP, [(1, 0), (2, 3)])
    third = jnp.where(inner, middle, outward)
    fourth = jnp.where(inner, across, last)
    blocks = [
        jnp.where(at == 0, values, jnp.where(at == 1, pair, fourth)),
        jnp.where(at == 1, values, jnp.where(at == 0, pair, third)),
        jnp.where(at == 2, values, jnp.where(at == 3, pair, third)),
        jnp.where(at == 3, values, jnp.where(at == 2, pair, fourth)),
    ]
    return jnp.concatenate(blocks, axis=0)


def xor_permute(values, bits):
    return lax.ppermute(values, ROWS, [(i, i ^ bits) for i in range(4)])


def swap_group(values):
    count = lax.axis_size(DP)
    return lax.ppermute(values, DP, [(i, i ^ 1) for i in range(count)])


PIECES = [(0, 1), (2, 2), (3, 3)]


def clamped(step, low, high):
    return jnp.clip(step - low, 0, high - low)


def take(arrays, table, layer, block, place, bound_dim, bound):
    count = len(arrays)
    rows, width = block

    def kernel(table_ref, *refs):
        step = pl.program_id(0)
        outs = refs[count:]
        for (low, high), out_ref in zip(PIECES, outs):

            @pl.when((step >= low) & (step <= high))
            def _():
                for i in range(count):
                    values = refs[i][...].reshape(rows, width)
                    if bound is not None:
                        first = place(2 + step, table_ref)[bound_dim] * block[bound_dim]
                        index = lax.broadcasted_iota(jnp.int32, (rows, width), bound_dim) + first
                        values = jnp.where(index < bound, values, jnp.zeros_like(values))
                    out_ref[i] = values

    if layer is None:
        in_spec = pl.BlockSpec(block, lambda i, s: place(2 + i, s))
    else:
        in_spec = pl.BlockSpec((1, *block), lambda i, s: (layer, *place(2 + i, s)))
    kind = arrays[0].dtype
    return pl.pallas_call(
        kernel,
        grid_spec=pltpu.PrefetchScalarGridSpec(
            num_scalar_prefetch=1,
            grid=(4,),
            in_specs=[in_spec] * count,
            out_specs=[
                pl.BlockSpec(
                    (count, rows, width), lambda i, s, low=low, high=high: (0, clamped(i, low, high), 0)
                )
                for low, high in PIECES
            ],
        ),
        out_shape=[
            jax.ShapeDtypeStruct((count, (high - low + 1) * rows, width), kind)
            for low, high in PIECES
        ],
    )(table, *arrays)


def join(arrays, parts, table, take_layer, block, take_place, bound_dim, bound, put_place, out_shape,
         dtype, layer=None, into=None):
    count = len(arrays)
    rows, width = block
    ranges = [(2, 3), (4, 4), (5, 5), (6, 6), (7, 7)]

    def kernel(table_ref, *refs):
        outs = refs[len(refs) - count :]
        piece = pl.program_id(0)

        @pl.when(piece <= 1)
        def _():
            for i in range(count):
                values = refs[i][...].reshape(rows, width)
                if bound is not None:
                    first = take_place(piece, table_ref)[bound_dim] * block[bound_dim]
                    index = lax.broadcasted_iota(jnp.int32, (rows, width), bound_dim) + first
                    values = jnp.where(index < bound, values, jnp.zeros_like(values))
                outs[i][...] = values.astype(dtype).reshape(outs[i].shape)

        for which, (low, high) in enumerate(ranges):

            @pl.when((piece >= low) & (piece <= high))
            def _():
                for i in range(count):
                    values = refs[count + which][i]
                    outs[i][...] = values.astype(dtype).reshape(outs[i].shape)

    if take_layer is None:
        own_spec = pl.BlockSpec(block, lambda i, s: take_place(jnp.minimum(i, 1), s))
    else:
        own_spec = pl.BlockSpec(
            (1, *block), lambda i, s: (take_layer, *take_place(jnp.minimum(i, 1), s))
        )
    in_specs = [own_spec] * count + [
        pl.BlockSpec(
            (count, rows, width), lambda i, s, low=low, high=high: (0, clamped(i, low, high), 0)
        )
        for low, high in ranges
    ]
    operands = [*arrays, *parts]
    aliases = {}
    if into is not None:
        for i, buffer in enumerate(into):
            aliases[1 + len(operands)] = i
            operands.append(buffer)
            in_specs.append(pl.BlockSpec(memory_space=pl.ANY))
    if layer is None:
        out_spec = pl.BlockSpec(block, lambda i, s: put_place(i, s))
    else:
        out_spec = pl.BlockSpec((1, *block), lambda i, s: (layer, *put_place(i, s)))
    return pl.pallas_call(
        kernel,
        grid_spec=pltpu.PrefetchScalarGridSpec(
            num_scalar_prefetch=1,
            grid=(8,),
            in_specs=in_specs,
            out_specs=[out_spec] * count,
        ),
        out_shape=[jax.ShapeDtypeStruct(out_shape, dtype)] * count,
        input_output_aliases=aliases,
    )(table, *operands)


def gated_all(normed, grads, gate_w, up_w, down_w):
    half, share = normed[0].shape[0], gate_w.shape[1]
    rows, width = 512, share // 3
    steps = half // rows

    def kernel(xn_ref, xf_ref, gn_ref, gf_ref, gate_ref, up_ref, down_ref, *outs):
        x_ref, g_ref, act_ref, dgate_ref, dup_ref = outs
        step = pl.program_id(0)

        @pl.when(step < steps)
        def _():
            x_ref[...] = xn_ref[...]
            g_ref[...] = gn_ref[...]

        @pl.when(step >= steps)
        def _():
            x_ref[...] = xf_ref[...]
            g_ref[...] = gf_ref[...]

        for tile in range(3):
            part = slice(tile * width, (tile + 1) * width)
            gate = mm(x_ref[...], gate_ref[:, part])
            up = mm(x_ref[...], up_ref[:, part])
            grad_units = mm_t(g_ref[...], down_ref[part, :])
            act_ref[:, part], dgate_ref[:, part], dup_ref[:, part] = gated(gate, up, grad_units)

    near_spec = pl.BlockSpec((rows, D), lambda i: (jnp.minimum(i, steps - 1), 0))
    far_spec = pl.BlockSpec((rows, D), lambda i: (jnp.maximum(i - steps, 0), 0))
    token_spec = pl.BlockSpec((rows, D), lambda i: (i, 0))
    out_spec = pl.BlockSpec((rows, share), lambda i: (i, 0))
    whole = [pl.BlockSpec(weight.shape, lambda i: (0, 0)) for weight in (gate_w, up_w, down_w)]
    tokens = 2 * half
    return pl.pallas_call(
        kernel,
        grid=(2 * steps,),
        in_specs=[near_spec, far_spec, near_spec, far_spec, *whole],
        out_specs=[token_spec] * 2 + [out_spec] * 3,
        out_shape=[jax.ShapeDtypeStruct((tokens, D), bf16)] * 2
        + [jax.ShapeDtypeStruct((tokens, share), bf16)] * 3,
        cost_estimate=pl.CostEstimate(
            flops=6 * tokens * share * D,
            bytes_accessed=2 * (4 * tokens * D + 3 * share * D + 3 * tokens * share),
            transcendentals=tokens * share,
        ),
    )(*normed, *grads, gate_w, up_w, down_w)


def gated(gate, up, grad_units):
    sigmoid_gate = jax.nn.sigmoid(gate)
    activated = (gate * sigmoid_gate * up).astype(bf16)
    grad_gate = grad_units * up * sigmoid_gate * (1.0 + gate * (1.0 - sigmoid_gate))
    grad_up = grad_units * gate * sigmoid_gate
    return activated, grad_gate.astype(bf16), grad_up.astype(bf16)


def body(hidden_in, attn_gain, w_qkv, b_qkv, w_out, mlp_gain, w_gate, w_up, w_down, out_grad):
    units = w_gate.shape[2]
    share = -(-units // (4 * 128)) * 128
    core = lax.axis_index(RK)
    column = lax.axis_index(CX)
    frame = attention_frame()
    everyone = lax.axis_size(DP) == 4

    place = lax.axis_index(RY) * 2 + core
    gains = lax.dynamic_update_slice(
        jnp.zeros((2 * LAYERS, D), f32),
        jnp.concatenate([attn_gain, mlp_gain], axis=0),
        (0, place * attn_gain.shape[1]),
    )
    gains = gains + swap_core(gains)
    gains = gains + swap_y(gains)
    attn_gain_full, mlp_gain_full = gains[:LAYERS], gains[LAYERS:]
    bias_other = swap_x(b_qkv)
    bias_here = jnp.where(core == column, b_qkv, bias_other)

    def tokens_whole(values):
        count, rows, width = values.shape
        blocks = values.reshape(count, 4, rows // 4, width)
        parts = []
        for bits in range(4):
            part = lax.dynamic_index_in_dim(blocks, place ^ bits, 1, keepdims=False)
            parts.append(part if bits == 0 else xor_permute(part, bits))
        parts = [jnp.where(core == 1, parts[i ^ 1], parts[i]) for i in range(4)]
        parts = [jnp.where(place >= 2, parts[i ^ 2], parts[i]) for i in range(4)]
        return jnp.concatenate(parts, axis=-1)

    def features_back(values):
        rows, width = values.shape[0], values.shape[1] // 4
        blocks = jnp.stack([values[:, i * width : (i + 1) * width] for i in range(4)])
        return lax.all_to_all(blocks, ROWS, 0, 0, tiled=True).reshape(4 * rows, width)

    def fetch_attention(layer):
        qkv_near = swap_diagonal(w_qkv[layer])
        out_near = swap_diagonal(w_out[layer])
        qkv_block = lax.all_gather(qkv_near, PLANE, axis=0)
        out_block = lax.all_gather(out_near, PLANE, axis=0)
        qkv_full = qkv_block.reshape(D, -1)
        out_full = jnp.concatenate([out_block[i] for i in range(4)], axis=1)
        return qkv_full, out_full

    half_d = D // 8
    unit_half = share // 2
    parity = lax.axis_index(DP) % 2
    sources = [place ^ bits for bits in range(4)]
    zero, one = jnp.int32(0), jnp.int32(1)
    take_table = jnp.stack(
        [sources[0], sources[0], sources[1], sources[1], sources[2], sources[3]]
        + [zero, one, zero, one, parity, parity]
    ).astype(jnp.int32)
    put_table = jnp.stack(
        [sources[i // 2] for i in range(8)] + [zero, one] * 2 + [parity, 1 - parity] * 2
    ).astype(jnp.int32)
    table = jnp.concatenate([take_table, put_table])

    def block_of(i, s):
        return s[i]

    def half_of(i, s):
        return s[6 + i]

    def put_block(i, s):
        return s[12 + i]

    def put_half(i, s):
        return s[20 + i]

    def exchange(sent):
        core_part, y_part, corner_part = sent
        y_mine = xor_permute(y_part, 2)
        corner_mine = xor_permute(corner_part, 3)
        return (
            swap_core(core_part), y_mine, swap_group(y_mine), corner_mine, swap_group(corner_mine)
        )

    def moved(arrays, from_layer, block, source, bound_dim, bound, target, shape, dtype,
              layer=None, into=None):
        sent = take(arrays, table, from_layer, block, source, bound_dim, bound)
        parts = exchange(sent)
        return join(
            arrays, parts, table, from_layer, block, source, bound_dim, bound, target, shape,
            dtype, layer, into,
        )

    def fetch_wide(layer):
        return moved(
            (w_gate, w_up), layer, (half_d, share),
            lambda i, s: (half_of(i, s), block_of(i, s)), 1, units,
            lambda i, s: (2 * put_block(i, s) + put_half(i, s), 0), (D, share), bf16,
        )

    def fetch_narrow(layer):
        return moved(
            (w_down,), layer, (unit_half, D // 4),
            lambda i, s: (2 * block_of(i, s) + half_of(i, s), 0), 0, units,
            lambda i, s: (put_half(i, s), put_block(i, s)), (share, D), bf16,
        )[0]

    def give_wide(grad, layer, into):
        return moved(
            (grad,), None, (half_d, share),
            lambda i, s: (2 * block_of(i, s) + half_of(i, s), 0), 0, None,
            lambda i, s: (put_half(i, s), put_block(i, s)), w_gate.shape, f32, layer, into,
        )

    def give_narrow(grad, layer, into):
        return moved(
            (grad,), None, (unit_half, D // 4),
            lambda i, s: (half_of(i, s), block_of(i, s)), 0, None,
            lambda i, s: (2 * put_block(i, s) + put_half(i, s), 0), w_down.shape, f32, layer, into,
        )

    def return_wide(grad):
        blocks = grad.astype(bf16).reshape(4, D // 4, share)
        arrived = lax.all_to_all(blocks, ROWS, 0, 0, tiled=True)
        spread = jnp.concatenate([arrived[i] for i in range(4)], axis=1)[:, :units]
        return sum_dp(spread)

    def return_narrow(grad):
        rows = grad.astype(bf16)
        blocks = jnp.stack([rows[:, i * (D // 4) : (i + 1) * (D // 4)] for i in range(4)])
        arrived = lax.all_to_all(blocks, ROWS, 0, 0, tiled=True)
        spread = arrived.reshape(4 * share, -1)[:units]
        return sum_dp(spread)

    def return_qkv(grad):
        blocks = grad.astype(bf16).reshape(4, D // 4, -1)
        summed = lax.psum_scatter(blocks, PLANE)
        return sum_dp(swap_diagonal(summed))

    def return_out(grad):
        rows = grad.astype(bf16)
        blocks = jnp.stack([rows[:, i * (D // 4) : (i + 1) * (D // 4)] for i in range(4)])
        summed = lax.psum_scatter(blocks, PLANE)
        return sum_dp(swap_diagonal(summed))

    def all_tokens(values, by_line):
        mine = values[: values.shape[0] // 2]
        if by_line:
            near = gather_line(mine)
        else:
            near = lax.all_gather(mine, DP, axis=0, tiled=True)
        return near, swap_core(near)

    def mlp_weight_grads(normed, grads, gate_w, up_w, down_w):
        normed, grads, activated, grad_gate, grad_up = gated_all(
            normed, grads, gate_w, up_w, down_w
        )
        return (
            t_mm(normed, grad_gate).astype(bf16),
            t_mm(normed, grad_up).astype(bf16),
            t_mm(activated, grads).astype(bf16),
        )

    both = tokens_whole(jnp.stack([hidden_in, out_grad]))
    resid = both[0].astype(f32)
    grad_start = both[1]
    own = resid.shape[0]

    saved = []
    for layer in range(LAYERS):
        qkv_full, out_full = fetch_attention(layer)
        gate_w, up_w = fetch_wide(layer)
        down_w = fetch_narrow(layer)
        normed_attn, scale_attn = norm_forward(resid, attn_gain_full[layer])
        pair_attn = jnp.concatenate([normed_attn, swap_core(normed_attn)], axis=0)
        qkv_rows = mm(pair_attn, qkv_full) + bias_here[layer][None, :]
        attended, kept = attention_forward(qkv_rows, frame)
        out_part = mm(attended, out_full)
        out_other = swap_core(out_part[own:].astype(bf16))
        middle = resid + out_part[:own] + out_other.astype(f32)
        normed_mlp, scale_mlp = norm_forward(middle, mlp_gain_full[layer])
        all_mlp = gather_eight(normed_mlp)
        gate = mm(all_mlp, gate_w)
        up = mm(all_mlp, up_w)
        activated = (jax.nn.silu(gate) * up).astype(bf16)
        saved.append(
            (resid, scale_attn, pair_attn, kept, attended, middle, scale_mlp, all_mlp, gate, up,
             activated, qkv_full, out_full, gate_w, up_w, down_w)
        )
        if layer < LAYERS - 1:
            resid = middle + scatter_eight(mm(activated, down_w))

    grad_resid = grad_start.astype(f32)
    grads = [None] * LAYERS
    small = [None] * LAYERS
    gate_out, up_out, narrow_out = None, None, None
    wide_parts, narrow_parts = [None] * LAYERS, [None] * LAYERS
    for layer in reversed(range(LAYERS)):
        (resid, scale_attn, pair_attn, kept, attended, middle, scale_mlp, all_mlp, gate, up,
         activated, qkv_full, out_full, gate_w, up_w, down_w) = saved[layer]
        all_grad = gather_eight(grad_resid.astype(bf16))
        if layer == 0:
            late = saved[LAYERS - 1]
            late_middle, late_units, _ = lax.optimization_barrier((late[5], late[10], all_grad))
            last_part = mm(late_units, late[15])
            resid_out = late_middle + scatter_eight(last_part)
            hidden_out = features_back(resid_out.astype(bf16))
        grad_units = mm_t(all_grad, down_w)
        _, grad_gate, grad_up = gated(gate, up, grad_units)
        grad_normed = scatter_eight(mm_t(grad_gate, gate_w) + mm_t(grad_up, up_w))
        if everyone:
            gate_grad, up_grad, down_grad = mlp_weight_grads(
                all_tokens(all_mlp, layer == LAYERS - 1),
                all_tokens(all_grad, layer < LAYERS - 1),
                gate_w, up_w, down_w,
            )
            narrow_out = give_narrow(down_grad, layer, narrow_out)
            gate_out = give_wide(gate_grad, layer, gate_out)
            up_out = give_wide(up_grad, layer, up_out)
        else:
            wide_parts[layer] = (
                return_wide(t_mm(all_mlp, grad_gate)),
                return_wide(t_mm(all_mlp, grad_up)),
            )
            narrow_parts[layer] = return_narrow(t_mm(activated, all_grad))
        grad_inner, mlp_gain_part = norm_backward(
            grad_normed, middle, scale_mlp, mlp_gain_full[layer]
        )
        grad_middle = grad_resid + grad_inner
        middle_round = grad_middle.astype(bf16)
        pair_grad = jnp.concatenate([middle_round, swap_core(middle_round)], axis=0)
        grad_heads = mm_t(pair_grad, out_full)
        out_grad_w = return_out(t_mm(attended, pair_grad))
        grad_qkv = attention_backward(grad_heads, kept, frame)
        bias_part = jnp.sum(grad_qkv, axis=0)
        qkv_round = grad_qkv.astype(bf16)
        grad_part = mm_t(qkv_round, qkv_full)
        grad_other = swap_core(grad_part[own:].astype(bf16))
        grad_normed_attn = grad_part[:own] + grad_other.astype(f32)
        qkv_grad_w = return_qkv(t_mm(pair_attn, qkv_round))
        grad_first, attn_gain_part = norm_backward(
            grad_normed_attn, resid, scale_attn, attn_gain_full[layer]
        )
        grad_resid = grad_middle + grad_first
        grads[layer] = (qkv_grad_w, out_grad_w)
        small[layer] = (attn_gain_part, mlp_gain_part, bias_part)
    in_grad = features_back(grad_resid.astype(bf16)).astype(f32)

    stacked = [
        jnp.stack([grads[layer][member].astype(f32) for layer in range(LAYERS)])
        for member in range(2)
    ]
    if everyone:
        stacked += [gate_out[0], up_out[0], narrow_out[0]]
    else:
        stacked += [
            jnp.stack([wide_parts[layer][member].astype(f32) for layer in range(LAYERS)])
            for member in range(2)
        ]
        stacked.append(jnp.stack([narrow_parts[layer].astype(f32) for layer in range(LAYERS)]))
    bias_stack = jnp.stack([small[layer][2] for layer in range(LAYERS)])
    bias_full = jnp.where(
        core == 0,
        jnp.concatenate([bias_stack, jnp.zeros_like(bias_stack)], axis=1),
        jnp.concatenate([jnp.zeros_like(bias_stack), bias_stack], axis=1),
    )
    packed = jnp.concatenate(
        [
            jnp.stack([small[layer][0] for layer in range(LAYERS)]),
            jnp.stack([small[layer][1] for layer in range(LAYERS)]),
            bias_full,
        ],
        axis=1,
    )
    packed = packed + swap_core(packed)
    packed = packed + swap_x(packed)
    packed = packed + swap_y(packed)
    if everyone:
        packed = sum_dp(packed)
    else:
        packed = lax.psum(packed, DP)
    row_width = attn_gain.shape[1]
    col_width = b_qkv.shape[1]
    row_place = place * row_width
    attn_gain_grad = lax.dynamic_slice_in_dim(packed[:, :D], row_place, row_width, 1)
    mlp_gain_grad = lax.dynamic_slice_in_dim(packed[:, D : 2 * D], row_place, row_width, 1)
    bias_grad = lax.dynamic_slice_in_dim(packed[:, 2 * D :], column * col_width, col_width, 1)
    return (
        hidden_out,
        in_grad,
        attn_gain_grad,
        stacked[0],
        bias_grad,
        stacked[1],
        mlp_gain_grad,
        stacked[2],
        stacked[3],
        stacked[4],
    )


def solution(mesh):
    fine = Mesh(
        mesh.devices.reshape(mesh.shape["dp"], 2, mesh.shape["rows"] // 2, mesh.shape["cols"]),
        (DP, RY, RK, CX),
    )
    in_specs = (
        P((DP, CX), ROWS),
        P(None, ROWS),
        P(None, ROWS, CX),
        P(None, CX),
        P(None, CX, ROWS),
        P(None, ROWS),
        P(None, ROWS, CX),
        P(None, ROWS, CX),
        P(None, CX, ROWS),
        P((DP, CX), ROWS),
    )
    out_specs = (
        P((DP, CX), ROWS),
        P((DP, CX), ROWS),
        P(None, ROWS),
        P(None, ROWS, CX),
        P(None, CX),
        P(None, CX, ROWS),
        P(None, ROWS),
        P(None, ROWS, CX),
        P(None, ROWS, CX),
        P(None, CX, ROWS),
    )

    return jax.shard_map(body, mesh=fine, in_specs=in_specs, out_specs=out_specs, check_vma=False)
```

profile of v0, /device:TPU:0, one launch (start us, length us, event | category | flops | bytes accessed | tf_op | source)
XLA Modules:
  0.0 1375.5 jit_solution(14543205992317267084)
XLA Ops:
  14.9 32.4 %collective-permute-start.7 = (f32[2,1024]{1,0:T(2,128)S(1)}, f32[2,1024]{1,0:T(2,128)S(1)}, u32[]{:S(2)}, u32[]{:S(2)}) collective-permute-start(f32[2,1024]{1,0:T(2,128)S(1)} %copy-done.112), channel_id=1, source_target_pairs={{0,1},{1,0},{2,3},{3,2},{4,5},{5,4},{6,7},{7,6},{8,9},{9,8},{10,11... | collective-permute-start | bytes 24584 | tf_op jit(solution)/shard_map/ppermute | solution.py:48
  51.6 11.7 collective-permute-done.4
  73.7 43.7 %all-gather.15.cloned.1.call-done = bf16[1536,1024]{1,0:T(8,128)(2,1)} async-done(((bf16[384,1024]{1,0:T(8,128)(2,1)}), bf16[1536,1024]{1,0:T(8,128)(2,1)}) %all-gather.15.cloned.1.call-update) | async-done | bytes 3145744 | tf_op jit(solution)/shard_map/all_gather | solution.py:418
  149.9 9.7 collective-permute-done.23.refs_4_
  166.6 32.2 %collective-permute-done.13 = bf16[48,1536]{1,0:T(8,128)(2,1)S(1)} collective-permute-done((bf16[48,1536]{1,0:T(8,128)(2,1)S(1)}, bf16[48,1536]{1,0:T(8,128)(2,1)S(1)}, u32[]{:S(2)}, u32[]{:S(2)}) %collective-permute-start.13) | collective-permute-done | bytes 147488 | tf_op jit(solution)/shard_map/ppermute | solution.py:52
  201.4 10.4 collective-permute-done.24.refs_5_
  222.5 12.2 collective-permute-done.17.refs_4_
  234.7 18.4 %collective-permute-done.19.refs_6_ = bf16[2,192,1152]{2,1,0:T(8,128)(2,1)} collective-permute-done((bf16[2,192,1152]{2,1,0:T(8,128)(2,1)}, bf16[2,192,1152]{2,1,0:T(8,128)(2,1)}, u32[]{:S(2)}, u32[]{:S(2)}) %collective-permute-start.19) | collective-permute-done | bytes 884768 | tf_op jit(solution)/shard_map/ppermute | solution.py:206
  253.2 8.9 shard_map.214
  288.8 13.1 collective-permute-start.52
  326.9 12.5 collective-permute-start.27
  342.5 10.7 collective-permute-start.46
  399.2 14.8 %collective-permute-done.40.refs_3_ = bf16[2,192,1152]{2,1,0:T(8,128)(2,1)} collective-permute-done((bf16[2,192,1152]{2,1,0:T(8,128)(2,1)}, bf16[2,192,1152]{2,1,0:T(8,128)(2,1)}, u32[]{:S(2)}, u32[]{:S(2)}) %collective-permute-start.40) | collective-permute-done | bytes 884768 | tf_op jit(solution)/shard_map/ppermute | solution.py:201
  414.7 16.4 %collective-permute-done.42.refs_5_ = bf16[2,192,1152]{2,1,0:T(8,128)(2,1)} collective-permute-done((bf16[2,192,1152]{2,1,0:T(8,128)(2,1)}, bf16[2,192,1152]{2,1,0:T(8,128)(2,1)}, u32[]{:S(2)}, u32[]{:S(2)}) %collective-permute-start.42) | collective-permute-done | bytes 884768 | tf_op jit(solution)/shard_map/ppermute | solution.py:201
  431.9 7.3 shard_map.220.down_ref
  441.6 7.7 fusion.208
  449.4 33.2 %collective-permute-done.41.refs_4_ = bf16[2,192,1152]{2,1,0:T(8,128)(2,1)} collective-permute-done((bf16[2,192,1152]{2,1,0:T(8,128)(2,1)}, bf16[2,192,1152]{2,1,0:T(8,128)(2,1)}, u32[]{:S(2)}, u32[]{:S(2)}) %collective-permute-start.41) | collective-permute-done | bytes 884768 | tf_op jit(solution)/shard_map/ppermute | solution.py:206
  482.6 42.5 %collective-permute-done.43.refs_6_ = bf16[2,192,1152]{2,1,0:T(8,128)(2,1)} collective-permute-done((bf16[2,192,1152]{2,1,0:T(8,128)(2,1)}, bf16[2,192,1152]{2,1,0:T(8,128)(2,1)}, u32[]{:S(2)}, u32[]{:S(2)}) %collective-permute-start.43) | collective-permute-done | bytes 884768 | tf_op jit(solution)/shard_map/ppermute | solution.py:206
  525.1 8.8 shard_map.218
  625.5 50.6 %collective-permute-done.112 = bf16[384,1536]{1,0:T(8,128)(2,1)} collective-permute-done((bf16[384,1536]{1,0:T(8,128)(2,1)}, bf16[384,1536]{1,0:T(8,128)(2,1)}, u32[]{:S(2)}, u32[]{:S(2)}) %collective-permute-start.112) | collective-permute-done | bytes 1179680 | tf_op jit(solution)/shard_map/ppermute | solution.py:184
  739.1 8.7 collective-permute-done.75
  759.7 11.5 collective-permute-done.114
  777.7 17.9 %collective-permute-done.101 = bf16[384,1536]{1,0:T(8,128)(2,1)} collective-permute-done((bf16[384,1536]{1,0:T(8,128)(2,1)}, bf16[384,1536]{1,0:T(8,128)(2,1)}, u32[]{:S(2)}, u32[]{:S(2)}) %collective-permute-start.101) | collective-permute-done | bytes 1179680 | tf_op jit(solution)/shard_map/ppermute | solution.py:184
  840.0 22.5 %collective-permute-start.81 = (f32[2,5120]{1,0:T(2,128)S(1)}, f32[2,5120]{1,0:T(2,128)S(1)}, u32[]{:S(2)}, u32[]{:S(2)}) collective-permute-start(f32[2,5120]{1,0:T(2,128)S(1)} %add.379), channel_id=1, source_target_pairs={{0,8},{24,16},{1,9},{25,17},{2,10},{26,18},{3,11},{27,19},{4,12},{... | collective-permute-start | bytes 122888 | tf_op jit(solution)/shard_map/ppermute | solution.py:173
  878.0 56.8 %shard_map.223 = (bf16[3072,1536]{1,0:T(8,128)(2,1)}, bf16[3072,1536]{1,0:T(8,128)(2,1)}, bf16[3072,1152]{1,0:T(8,128)(2,1)}, bf16[3072,1152]{1,0:T(8,128)(2,1)}, bf16[3072,1152]{1,0:T(8,128)(2,1)}) custom-call(bf16[1536,1536]{1,0:T(8,128)(2,1)} %pad_maximum_fusion.1.xn_ref, bf16[1536,1536]{1,0:T(8,128)(2,1)} %collective-permute-done.117.xf_ref, ...), custom_call_target="tpu_custom_call" | custom-call | flops 32614907904 | bytes 69599232 | tf_op jit(solution)/shard_map/pallas_call | solution.py:356
  936.7 17.9 %convolution_convert_fusion.2.refs_0_ = bf16[1536,1152]{1,0:T(8,128)(2,1)} fusion(bf16[3072,1536]{1,0:T(8,128)(2,1)} %get-tuple-element.79, bf16[3072,1152]{1,0:T(8,128)(2,1)} %get-tuple-element.88), kind=kOutput, calls=%fused_computation.4 | convolution fusion | flops 10873405440 | bytes 20054016 | tf_op jit(solution)/shard_map/dot_general | solution.py:40
  964.4 16.8 %convolution_convert_fusion.refs_0_ = bf16[1152,1536]{1,0:T(8,128)(2,1)} fusion(bf16[3072,1152]{1,0:T(8,128)(2,1)} %get-tuple-element.97, bf16[3072,1536]{1,0:T(8,128)(2,1)} %get-tuple-element.98), kind=kOutput, calls=%fused_computation.2 | convolution fusion | flops 10873405440 | bytes 20054016 | tf_op jit(solution)/shard_map/dot_general | solution.py:40
  982.1 10.6 collective-permute-done.89
  993.8 14.4 %convolution_convert_fusion.4.refs_0_ = bf16[1536,1152]{1,0:T(8,128)(2,1)} fusion(bf16[3072,1536]{1,0:T(8,128)(2,1)S(1)} %bitcast.291, bf16[3072,1152]{1,0:T(8,128)(2,1)S(1)} %bitcast.293), kind=kOutput, calls=%fused_computation.6 | convolution fusion | flops 10873405440 | bytes 20054016 | tf_op jit(solution)/shard_map/dot_general | solution.py:40
  1031.1 9.7 collective-permute-done.120.refs_2_
  1040.8 7.6 collective-permute-done.122.refs_4_
  1050.1 56.5 %shard_map.221 = (bf16[3072,1536]{1,0:T(8,128)(2,1)}, bf16[3072,1536]{1,0:T(8,128)(2,1)}, bf16[3072,1152]{1,0:T(8,128)(2,1)}, bf16[3072,1152]{1,0:T(8,128)(2,1)}, bf16[3072,1152]{1,0:T(8,128)(2,1)}) custom-call(bf16[1536,1536]{1,0:T(8,128)(2,1)} %all-gather.11.cloned.1.call-done.xn_ref, bf16[1536,1536]{1,0:T(8,128)(2,1)} %collective-permute-done.100.xf_ref, ...), custom_call_target="tpu_custom_call" | custom-call | flops 32614907904 | bytes 69599232 | tf_op jit(solution)/shard_map/pallas_call | solution.py:356
  1115.6 17.9 %convolution_convert_fusion.5.refs_0_ = bf16[1536,1152]{1,0:T(8,128)(2,1)} fusion(bf16[3072,1536]{1,0:T(8,128)(2,1)} %get-tuple-element.74, bf16[3072,1152]{1,0:T(8,128)(2,1)} %get-tuple-element.75), kind=kOutput, calls=%fused_computation.7 | convolution fusion | flops 10873405440 | bytes 20054016 | tf_op jit(solution)/shard_map/dot_general | solution.py:40
  1143.6 7.8 collective-permute-done.123.refs_5_
  1152.6 8.2 collective-permute-done.141.refs_3_
  1160.8 7.4 collective-permute-start.84
  1168.2 18.1 %convolution_convert_fusion.3.refs_0_ = bf16[1536,1152]{1,0:T(8,128)(2,1)} fusion(bf16[3072,1536]{1,0:T(8,128)(2,1)} %get-tuple-element.74, bf16[3072,1152]{1,0:T(8,128)(2,1)} %get-tuple-element.84), kind=kOutput, calls=%fused_computation.5 | convolution fusion | flops 10873405440 | bytes 20054016 | tf_op jit(solution)/shard_map/dot_general | solution.py:40
  1204.8 16.9 %convolution_convert_fusion.1.refs_0_ = bf16[1152,1536]{1,0:T(8,128)(2,1)} fusion(bf16[3072,1152]{1,0:T(8,128)(2,1)} %get-tuple-element.92, bf16[3072,1536]{1,0:T(8,128)(2,1)} %get-tuple-element.93), kind=kOutput, calls=%fused_computation.3 | convolution fusion | flops 10873405440 | bytes 20054016 | tf_op jit(solution)/shard_map/dot_general | solution.py:40
  1238.4 11.5 collective-permute-done.135.refs_2_
  1260.2 7.4 shard_map.233.refs_6_
  1267.5 7.4 shard_map.225.refs_6_
  1274.9 7.4 shard_map.229.refs_6_
  1296.2 9.5 collective-permute-done.136.refs_3_
  1305.7 9.5 collective-permute-done.138.refs_5_
  1318.5 7.4 shard_map.234
  1325.9 7.4 shard_map.226
  1337.4 9.5 collective-permute-done.128.refs_5_
  1346.8 7.4 shard_map.230
  (809 shorter events, 548.0 us)
Async XLA Ops:
  8.0 62.8 %all-gather.17.cloned.1.call-start = ((), (), s32[]{:S(2)}) async-start(), calls=%async_computation.9 | async-start | bytes 2949120 | tf_op jit(solution)/shard_map/all_gather | solution.py:419
  12.1 105.3 %all-gather.15.cloned.1.call-start = ((), (), s32[]{:S(2)}) async-start(), calls=%async_computation.8 | async-start | bytes 3932160 | tf_op jit(solution)/shard_map/all_gather | solution.py:418
  14.8 346.0 %all-gather.21.cloned.1.call-start = ((), (), s32[]{:S(2)}) async-start(), calls=%async_computation.11 | async-start | bytes 2949120 | tf_op jit(solution)/shard_map/all_gather | solution.py:419
  144.7 67.1 %collective-permute-start.16 = (bf16[2,192,1152]{2,1,0:T(8,128)(2,1)}, bf16[2,192,1152]{2,1,0:T(8,128)(2,1)}, u32[]{:S(2)}, u32[]{:S(2)}) collective-permute-start(bf16[2,192,1152]{2,1,0:T(8,128)(2,1)} %get-tuple-element.57), channel_id=1, source_target_pairs={{0,4},{2,6},{4,0},{6,2},{1,5},{3,7},{5,1},{7,3},{8,12},{10,14},{12... | collective-permute-start | bytes 2654216 | tf_op jit(solution)/shard_map/ppermute | solution.py:201
  145.3 68.0 %collective-permute-start.18 = (bf16[2,192,1152]{2,1,0:T(8,128)(2,1)}, bf16[2,192,1152]{2,1,0:T(8,128)(2,1)}, u32[]{:S(2)}, u32[]{:S(2)}) collective-permute-start(bf16[2,192,1152]{2,1,0:T(8,128)(2,1)} %get-tuple-element.58), channel_id=1, source_target_pairs={{0,6},{2,4},{4,2},{6,0},{1,7},{3,5},{5,3},{7,1},{8,14},{10,12},{12... | collective-permute-start | bytes 2654216 | tf_op jit(solution)/shard_map/ppermute | solution.py:201
  148.4 104.7 %collective-permute-start.15 = (bf16[2,384,1152]{2,1,0:T(8,128)(2,1)}, bf16[2,384,1152]{2,1,0:T(8,128)(2,1)}, u32[]{:S(2)}, u32[]{:S(2)}) collective-permute-start(bf16[2,384,1152]{2,1,0:T(8,128)(2,1)} %get-tuple-element.56), channel_id=1, source_target_pairs={{0,2},{2,0},{1,3},{3,1},{4,6},{6,4},{5,7},{7,5},{8,10},{10,8},{9,1... | collective-permute-start | bytes 5308424 | tf_op jit(solution)/shard_map/ppermute | solution.py:44
  201.0 61.0 %collective-permute-start.14 = (bf16[384,1536]{1,0:T(8,128)(2,1)}, bf16[384,1536]{1,0:T(8,128)(2,1)}, u32[]{:S(2)}, u32[]{:S(2)}) collective-permute-start(bf16[384,1536]{1,0:T(8,128)(2,1)} %get-tuple-element.248), channel_id=1, source_target_pairs={{0,2},{2,0},{1,3},{3,1},{4,6},{6,4},{5,7},{7,5},{8,10},{10,8},{9,1... | collective-permute-start | bytes 3538952 | tf_op jit(solution)/shard_map/ppermute | solution.py:44
  214.0 150.0 %all-gather.19.cloned.1.call-start = ((), (), s32[]{:S(2)}) async-start(), calls=%async_computation.10 | async-start | bytes 3932160 | tf_op jit(solution)/shard_map/all_gather | solution.py:418
  282.2 432.2 %all-gather.13.cloned.1.call-start = ((), (), s32[]{:S(2)}) async-start(), calls=%async_computation.7 | async-start | bytes 5898240 | tf_op jit(solution)/shard_map/all_gather | solution.py:524
  287.2 55.2 %collective-permute-start.50 = (bf16[1,576,384]{2,1,0:T(8,128)(2,1)}, bf16[1,576,384]{2,1,0:T(8,128)(2,1)}, u32[]{:S(2)}, u32[]{:S(2)}) collective-permute-start(bf16[1,576,384]{2,1,0:T(8,128)(2,1)} %get-tuple-element.70), channel_id=1, source_target_pairs={{0,4},{2,6},{4,0},{6,2},{1,5},{3,7},{5,1},{7,3},{8,12},{10,14},{12... | collective-permute-start | bytes 1327112 | tf_op jit(solution)/shard_map/ppermute | solution.py:201
  288.8 64.4 %collective-permute-start.52 = (bf16[1,576,384]{2,1,0:T(8,128)(2,1)}, bf16[1,576,384]{2,1,0:T(8,128)(2,1)}, u32[]{:S(2)}, u32[]{:S(2)}) collective-permute-start(bf16[1,576,384]{2,1,0:T(8,128)(2,1)} %get-tuple-element.71), channel_id=1, source_target_pairs={{0,6},{2,4},{4,2},{6,0},{1,7},{3,5},{5,3},{7,1},{8,14},{10,12},{12... | collective-permute-start | bytes 1327112 | tf_op jit(solution)/shard_map/ppermute | solution.py:201
  379.7 59.5 %collective-permute-start.48 = (bf16[384,1536]{1,0:T(8,128)(2,1)}, bf16[384,1536]{1,0:T(8,128)(2,1)}, u32[]{:S(2)}, u32[]{:S(2)}) collective-permute-start(bf16[384,1536]{1,0:T(8,128)(2,1)} %get-tuple-element.240), channel_id=1, source_target_pairs={{0,2},{2,0},{1,3},{3,1},{4,6},{6,4},{5,7},{7,5},{8,10},{10,8},{9,1... | collective-permute-start | bytes 3538952 | tf_op jit(solution)/shard_map/ppermute | solution.py:44
  393.9 131.2 %collective-permute-start.39 = (bf16[2,384,1152]{2,1,0:T(8,128)(2,1)}, bf16[2,384,1152]{2,1,0:T(8,128)(2,1)}, u32[]{:S(2)}, u32[]{:S(2)}) collective-permute-start(bf16[2,384,1152]{2,1,0:T(8,128)(2,1)} %get-tuple-element.64), channel_id=1, source_target_pairs={{0,2},{2,0},{1,3},{3,1},{4,6},{6,4},{5,7},{7,5},{8,10},{10,8},{9,1... | collective-permute-start | bytes 5308424 | tf_op jit(solution)/shard_map/ppermute | solution.py:44
  399.2 134.8 %collective-permute-start.38 = (bf16[384,1536]{1,0:T(8,128)(2,1)}, bf16[384,1536]{1,0:T(8,128)(2,1)}, u32[]{:S(2)}, u32[]{:S(2)}) collective-permute-start(bf16[384,1536]{1,0:T(8,128)(2,1)} %get-tuple-element.244), channel_id=1, source_target_pairs={{0,2},{2,0},{1,3},{3,1},{4,6},{6,4},{5,7},{7,5},{8,10},{10,8},{9,1... | collective-permute-start | bytes 3538952 | tf_op jit(solution)/shard_map/ppermute | solution.py:44
  399.2 440.3 %all-gather.11.cloned.1.call-start = ((), (), s32[]{:S(2)}) async-start(), calls=%async_computation.6 | async-start | bytes 5898240 | tf_op jit(solution)/shard_map/all_gather | solution.py:524
  414.1 68.5 %collective-permute-start.41 = (bf16[2,192,1152]{2,1,0:T(8,128)(2,1)}, bf16[2,192,1152]{2,1,0:T(8,128)(2,1)}, u32[]{:S(2)}, u32[]{:S(2)}) collective-permute-start(bf16[2,192,1152]{2,1,0:T(8,128)(2,1)} %collective-permute-done.40.refs_3_), channel_id=1, source_target_pairs={{0,8},{8,0},{16,24},{24,16},{1,9},{9,1},{17,25},{25,17},{2,10},{10... | collective-permute-start | bytes 2654216 | tf_op jit(solution)/shard_map/ppermute | solution.py:206
  431.2 93.9 %collective-permute-start.43 = (bf16[2,192,1152]{2,1,0:T(8,128)(2,1)}, bf16[2,192,1152]{2,1,0:T(8,128)(2,1)}, u32[]{:S(2)}, u32[]{:S(2)}) collective-permute-start(bf16[2,192,1152]{2,1,0:T(8,128)(2,1)} %collective-permute-done.42.refs_5_), channel_id=1, source_target_pairs={{0,8},{8,0},{16,24},{24,16},{1,9},{9,1},{17,25},{25,17},{2,10},{10... | collective-permute-start | bytes 2654216 | tf_op jit(solution)/shard_map/ppermute | solution.py:206
  565.6 310.7 %reduce-scatter.19.cloned.1.call-start = ((), (), s32[]{:S(2)}) async-start(), calls=%async_computation.15 | async-start | bytes 2949120
  601.7 74.4 %collective-permute-start.112 = (bf16[384,1536]{1,0:T(8,128)(2,1)}, bf16[384,1536]{1,0:T(8,128)(2,1)}, u32[]{:S(2)}, u32[]{:S(2)}) collective-permute-start(bf16[384,1536]{1,0:T(8,128)(2,1)} %get-tuple-element.244), channel_id=1, source_target_pairs={{0,8},{8,0},{16,24},{24,16},{1,9},{9,1},{17,25},{25,17},{2,10},{10... | collective-permute-start | bytes 3538952 | tf_op jit(solution)/shard_map/ppermute | solution.py:184
  621.6 56.3 %collective-permute-start.65 = (bf16[384,1536]{1,0:T(8,128)(2,1)}, bf16[384,1536]{1,0:T(8,128)(2,1)}, u32[]{:S(2)}, u32[]{:S(2)}) collective-permute-start(bf16[384,1536]{1,0:T(8,128)(2,1)} %get-tuple-element.236), channel_id=1, source_target_pairs={{0,2},{2,0},{1,3},{3,1},{4,6},{6,4},{5,7},{7,5},{8,10},{10,8},{9,1... | collective-permute-start | bytes 3538952 | tf_op jit(solution)/shard_map/ppermute | solution.py:44
  623.8 311.1 %reduce-scatter.15.cloned.1.call-start = ((), (), s32[]{:S(2)}) async-start(), calls=%async_computation.13 | async-start | bytes 3932160
  623.8 91.1 %collective-permute-start.115 = (bf16[384,1536]{1,0:T(8,128)(2,1)}, bf16[384,1536]{1,0:T(8,128)(2,1)}, u32[]{:S(2)}, u32[]{:S(2)}) collective-permute-start(bf16[384,1536]{1,0:T(8,128)(2,1)} %get-tuple-element.244), channel_id=1, source_target_pairs={{8,16},{16,8},{9,17},{17,9},{10,18},{18,10},{11,19},{19,11},{12,20... | collective-permute-start | bytes 3538952 | tf_op jit(solution)/shard_map/ppermute | solution.py:185
  705.2 436.6 %reduce-scatter.17.cloned.1.call-start = ((), (), s32[]{:S(2)}) async-start(), calls=%async_computation.14 | async-start | bytes 2949120
  714.4 163.6 %collective-permute-start.118 = (bf16[1536,1536]{1,0:T(8,128)(2,1)}, bf16[1536,1536]{1,0:T(8,128)(2,1)}, u32[]{:S(2)}, u32[]{:S(2)}) collective-permute-start(bf16[1536,1536]{1,0:T(8,128)(2,1)} %all-gather.13.cloned.1.call-done.gn_ref), channel_id=1, source_target_pairs={{0,2},{2,0},{1,3},{3,1},{4,6},{6,4},{5,7},{7,5},{8,10},{10,8},{9,1... | collective-permute-start | bytes 14155784 | tf_op jit(solution)/shard_map/ppermute | solution.py:44
  716.2 55.0 %collective-permute-start.114 = (bf16[384,1536]{1,0:T(8,128)(2,1)}, bf16[384,1536]{1,0:T(8,128)(2,1)}, u32[]{:S(2)}, u32[]{:S(2)}) collective-permute-start(bf16[384,1536]{1,0:T(8,128)(2,1)} %collective-permute-done.113), channel_id=1, source_target_pairs={{8,0},{16,24},{9,1},{17,25},{10,2},{18,26},{11,3},{19,27},{12,4},{... | collective-permute-start | bytes 3538952 | tf_op jit(solution)/shard_map/ppermute | solution.py:188
  747.8 47.7 %collective-permute-start.101 = (bf16[384,1536]{1,0:T(8,128)(2,1)}, bf16[384,1536]{1,0:T(8,128)(2,1)}, u32[]{:S(2)}, u32[]{:S(2)}) collective-permute-start(bf16[384,1536]{1,0:T(8,128)(2,1)} %get-tuple-element.236), channel_id=1, source_target_pairs={{0,8},{8,0},{16,24},{24,16},{1,9},{9,1},{17,25},{25,17},{2,10},{10... | collective-permute-start | bytes 3538952 | tf_op jit(solution)/shard_map/ppermute | solution.py:184
  803.4 357.4 %reduce-scatter.13.cloned.1.call-start = ((), (), s32[]{:S(2)}) async-start(), calls=%async_computation.12 | async-start | bytes 3932160
  807.8 70.3 %collective-permute-start.117 = (bf16[1536,1536]{1,0:T(8,128)(2,1)}, bf16[1536,1536]{1,0:T(8,128)(2,1)}, u32[]{:S(2)}, u32[]{:S(2)}) collective-permute-start(bf16[1536,1536]{1,0:T(8,128)(2,1)} %pad_maximum_fusion.1.xn_ref), channel_id=1, source_target_pairs={{0,2},{2,0},{1,3},{3,1},{4,6},{6,4},{5,7},{7,5},{8,10},{10,8},{9,1... | collective-permute-start | bytes 14155784 | tf_op jit(solution)/shard_map/ppermute | solution.py:44
  809.5 54.2 %collective-permute-start.103 = (bf16[384,1536]{1,0:T(8,128)(2,1)}, bf16[384,1536]{1,0:T(8,128)(2,1)}, u32[]{:S(2)}, u32[]{:S(2)}) collective-permute-start(bf16[384,1536]{1,0:T(8,128)(2,1)} %collective-permute-done.102), channel_id=1, source_target_pairs={{8,0},{16,24},{9,1},{17,25},{10,2},{18,26},{11,3},{19,27},{12,4},{... | collective-permute-start | bytes 3538952 | tf_op jit(solution)/shard_map/ppermute | solution.py:188
  839.5 178.0 %collective-permute-start.100 = (bf16[1536,1536]{1,0:T(8,128)(2,1)}, bf16[1536,1536]{1,0:T(8,128)(2,1)}, u32[]{:S(2)}, u32[]{:S(2)}) collective-permute-start(bf16[1536,1536]{1,0:T(8,128)(2,1)} %all-gather.11.cloned.1.call-done.xn_ref), channel_id=1, source_target_pairs={{0,2},{2,0},{1,3},{3,1},{4,6},{6,4},{5,7},{7,5},{8,10},{10,8},{9,1... | collective-permute-start | bytes 14155784 | tf_op jit(solution)/shard_map/ppermute | solution.py:44
  869.8 179.9 %collective-permute-start.106 = (bf16[1536,1536]{1,0:T(8,128)(2,1)}, bf16[1536,1536]{1,0:T(8,128)(2,1)}, u32[]{:S(2)}, u32[]{:S(2)}) collective-permute-start(bf16[1536,1536]{1,0:T(8,128)(2,1)} %pad_maximum_fusion.gn_ref), channel_id=1, source_target_pairs={{0,2},{2,0},{1,3},{3,1},{4,6},{6,4},{5,7},{7,5},{8,10},{10,8},{9,1... | collective-permute-start | bytes 14155784 | tf_op jit(solution)/shard_map/ppermute | solution.py:44
  876.3 84.8 %collective-permute-start.96 = (bf16[768,384]{1,0:T(8,128)(2,1)}, bf16[768,384]{1,0:T(8,128)(2,1)S(1)}, u32[]{:S(2)}, u32[]{:S(2)}) collective-permute-start(bf16[768,384]{1,0:T(8,128)(2,1)} %bitcast.288), channel_id=1, source_target_pairs={{0,0},{1,2},{2,1},{3,3},{4,4},{5,6},{6,5},{7,7},{8,8},{9,10},{10,9... | collective-permute-start | bytes 1769480 | tf_op jit(solution)/shard_map/ppermute | solution.py:56
  959.2 62.4 %collective-permute-start.130 = (bf16[1,192,1152]{2,1,0:T(8,128)(2,1)}, bf16[1,192,1152]{2,1,0:T(8,128)(2,1)}, u32[]{:S(2)}, u32[]{:S(2)}) collective-permute-start(bf16[1,192,1152]{2,1,0:T(8,128)(2,1)} %get-tuple-element.90), channel_id=1, source_target_pairs={{0,4},{2,6},{4,0},{6,2},{1,5},{3,7},{5,1},{7,3},{8,12},{10,14},{12... | collective-permute-start | bytes 1327112 | tf_op jit(solution)/shard_map/ppermute | solution.py:201
  1021.7 90.0 %collective-permute-start.129 = (bf16[1,384,1152]{2,1,0:T(8,128)(2,1)}, bf16[1,384,1152]{2,1,0:T(8,128)(2,1)}, u32[]{:S(2)}, u32[]{:S(2)}) collective-permute-start(bf16[1,384,1152]{2,1,0:T(8,128)(2,1)} %get-tuple-element.89), channel_id=1, source_target_pairs={{0,2},{2,0},{1,3},{3,1},{4,6},{6,4},{5,7},{7,5},{8,10},{10,8},{9,1... | collective-permute-start | bytes 2654216 | tf_op jit(solution)/shard_map/ppermute | solution.py:44
  1029.4 84.2 %collective-permute-start.119 = (bf16[1,384,1152]{2,1,0:T(8,128)(2,1)}, bf16[1,384,1152]{2,1,0:T(8,128)(2,1)}, u32[]{:S(2)}, u32[]{:S(2)}) collective-permute-start(bf16[1,384,1152]{2,1,0:T(8,128)(2,1)} %get-tuple-element.81), channel_id=1, source_target_pairs={{0,2},{2,0},{1,3},{3,1},{4,6},{6,4},{5,7},{7,5},{8,10},{10,8},{9,1... | collective-permute-start | bytes 2654216 | tf_op jit(solution)/shard_map/ppermute | solution.py:44
  1040.7 65.8 %collective-permute-start.140 = (bf16[1,576,384]{2,1,0:T(8,128)(2,1)}, bf16[1,576,384]{2,1,0:T(8,128)(2,1)}, u32[]{:S(2)}, u32[]{:S(2)}) collective-permute-start(bf16[1,576,384]{2,1,0:T(8,128)(2,1)} %get-tuple-element.100), channel_id=1, source_target_pairs={{0,4},{2,6},{4,0},{6,2},{1,5},{3,7},{5,1},{7,3},{8,12},{10,14},{12... | collective-permute-start | bytes 1327112 | tf_op jit(solution)/shard_map/ppermute | solution.py:201
  1048.4 63.2 %collective-permute-start.142 = (bf16[1,576,384]{2,1,0:T(8,128)(2,1)}, bf16[1,576,384]{2,1,0:T(8,128)(2,1)}, u32[]{:S(2)}, u32[]{:S(2)}) collective-permute-start(bf16[1,576,384]{2,1,0:T(8,128)(2,1)} %get-tuple-element.101), channel_id=1, source_target_pairs={{0,6},{2,4},{4,2},{6,0},{1,7},{3,5},{5,3},{7,1},{8,14},{10,12},{12... | collective-permute-start | bytes 1327112 | tf_op jit(solution)/shard_map/ppermute | solution.py:201
  1049.7 64.0 %collective-permute-start.139 = (bf16[1,1152,384]{2,1,0:T(8,128)(2,1)}, bf16[1,1152,384]{2,1,0:T(8,128)(2,1)}, u32[]{:S(2)}, u32[]{:S(2)}) collective-permute-start(bf16[1,1152,384]{2,1,0:T(8,128)(2,1)} %get-tuple-element.99), channel_id=1, source_target_pairs={{0,2},{2,0},{1,3},{3,1},{4,6},{6,4},{5,7},{7,5},{8,10},{10,8},{9,1... | collective-permute-start | bytes 2654216 | tf_op jit(solution)/shard_map/ppermute | solution.py:44
  1113.7 47.1 %collective-permute-start.141 = (bf16[1,576,384]{2,1,0:T(8,128)(2,1)}, bf16[1,576,384]{2,1,0:T(8,128)(2,1)}, u32[]{:S(2)}, u32[]{:S(2)}) collective-permute-start(bf16[1,576,384]{2,1,0:T(8,128)(2,1)} %collective-permute-done.140.refs_2_), channel_id=1, source_target_pairs={{0,8},{8,0},{16,24},{24,16},{1,9},{9,1},{17,25},{25,17},{2,10},{10... | collective-permute-start | bytes 1327112 | tf_op jit(solution)/shard_map/ppermute | solution.py:206
  1133.6 62.1 %collective-permute-start.143 = (bf16[1,576,384]{2,1,0:T(8,128)(2,1)}, bf16[1,576,384]{2,1,0:T(8,128)(2,1)}, u32[]{:S(2)}, u32[]{:S(2)}) collective-permute-start(bf16[1,576,384]{2,1,0:T(8,128)(2,1)} %collective-permute-done.142.refs_4_), channel_id=1, source_target_pairs={{0,8},{8,0},{16,24},{24,16},{1,9},{9,1},{17,25},{25,17},{2,10},{10... | collective-permute-start | bytes 1327112 | tf_op jit(solution)/shard_map/ppermute | solution.py:206
  1133.7 63.7 %collective-permute-start.99 = (bf16[768,384]{1,0:T(8,128)(2,1)S(1)}, bf16[768,384]{1,0:T(8,128)(2,1)}, u32[]{:S(2)}, u32[]{:S(2)}) collective-permute-start(bf16[768,384]{1,0:T(8,128)(2,1)S(1)} %add_convert_fusion.4), channel_id=1, source_target_pairs={{8,0},{16,24},{9,1},{17,25},{10,2},{18,26},{11,3},{19,27},{12,4},{... | collective-permute-start | bytes 1769480 | tf_op jit(solution)/shard_map/ppermute | solution.py:177
  1141.9 55.5 %collective-permute-start.92 = (bf16[768,384]{1,0:T(8,128)(2,1)}, bf16[768,384]{1,0:T(8,128)(2,1)S(1)}, u32[]{:S(2)}, u32[]{:S(2)}) collective-permute-start(bf16[768,384]{1,0:T(8,128)(2,1)} %bitcast.289), channel_id=1, source_target_pairs={{0,0},{1,2},{2,1},{3,3},{4,4},{5,6},{6,5},{7,7},{8,8},{9,10},{10,9... | collective-permute-start | bytes 1769480 | tf_op jit(solution)/shard_map/ppermute | solution.py:56
  1151.3 47.8 %collective-permute-start.91 = (bf16[384,1024]{1,0:T(8,128)(2,1)S(1)}, bf16[384,1024]{1,0:T(8,128)(2,1)S(1)}, u32[]{:S(2)}, u32[]{:S(2)}) collective-permute-start(bf16[384,1024]{1,0:T(8,128)(2,1)S(1)} %add_convert_fusion), channel_id=1, source_target_pairs={{8,0},{16,24},{9,1},{17,25},{10,2},{18,26},{11,3},{19,27},{12,4},{... | collective-permute-start | bytes 2359304 | tf_op jit(solution)/shard_map/ppermute | solution.py:177
  1230.9 51.4 %collective-permute-start.107 = (bf16[1,384,1152]{2,1,0:T(8,128)(2,1)}, bf16[1,384,1152]{2,1,0:T(8,128)(2,1)}, u32[]{:S(2)}, u32[]{:S(2)}) collective-permute-start(bf16[1,384,1152]{2,1,0:T(8,128)(2,1)} %get-tuple-element.76), channel_id=1, source_target_pairs={{0,2},{2,0},{1,3},{3,1},{4,6},{6,4},{5,7},{7,5},{8,10},{10,8},{9,1... | collective-permute-start | bytes 2654216 | tf_op jit(solution)/shard_map/ppermute | solution.py:44
  1232.0 50.9 %collective-permute-start.134 = (bf16[1,1152,384]{2,1,0:T(8,128)(2,1)}, bf16[1,1152,384]{2,1,0:T(8,128)(2,1)}, u32[]{:S(2)}, u32[]{:S(2)}) collective-permute-start(bf16[1,1152,384]{2,1,0:T(8,128)(2,1)} %get-tuple-element.94), channel_id=1, source_target_pairs={{0,2},{2,0},{1,3},{3,1},{4,6},{6,4},{5,7},{7,5},{8,10},{10,8},{9,1... | collective-permute-start | bytes 2654216 | tf_op jit(solution)/shard_map/ppermute | solution.py:44
  1282.3 51.0 %collective-permute-start.124 = (bf16[1,384,1152]{2,1,0:T(8,128)(2,1)}, bf16[1,384,1152]{2,1,0:T(8,128)(2,1)}, u32[]{:S(2)}, u32[]{:S(2)}) collective-permute-start(bf16[1,384,1152]{2,1,0:T(8,128)(2,1)} %get-tuple-element.85), channel_id=1, source_target_pairs={{0,2},{2,0},{1,3},{3,1},{4,6},{6,4},{5,7},{7,5},{8,10},{10,8},{9,1... | collective-permute-start | bytes 2654216 | tf_op jit(solution)/shard_map/ppermute | solution.py:44
  1287.1 67.2 %collective-permute-start.95 = (bf16[768,384]{1,0:T(8,128)(2,1)}, bf16[768,384]{1,0:T(8,128)(2,1)}, u32[]{:S(2)}, u32[]{:S(2)}) collective-permute-start(bf16[768,384]{1,0:T(8,128)(2,1)} %add_convert_fusion.6), channel_id=1, source_target_pairs={{8,0},{16,24},{9,1},{17,25},{10,2},{18,26},{11,3},{19,27},{12,4},{... | collective-permute-start | bytes 1769480 | tf_op jit(solution)/shard_map/ppermute | solution.py:177
  1315.1 47.7 %collective-permute-start.87 = (bf16[384,1024]{1,0:T(8,128)(2,1)S(1)}, bf16[384,1024]{1,0:T(8,128)(2,1)}, u32[]{:S(2)}, u32[]{:S(2)}) collective-permute-start(bf16[384,1024]{1,0:T(8,128)(2,1)S(1)} %add_convert_fusion.2), channel_id=1, source_target_pairs={{8,0},{16,24},{9,1},{17,25},{10,2},{18,26},{11,3},{19,27},{12,4},{... | collective-permute-start | bytes 2359304 | tf_op jit(solution)/shard_map/ppermute | solution.py:177
  (256 other events, 4244.6 us)
Sparse Core Ops, SparseCore 0:
  12.2 58.5 all-gather.16
  73.2 44.1 all-gather.14
  214.1 37.4 all-gather.20
  282.3 79.5 all-gather.18
  623.9 36.5 reduce-scatter.18
  705.3 51.3 reduce-scatter.14
  759.8 37.4 reduce-scatter.16
  827.0 70.5 reduce-scatter.12
Sparse Core Ops, SparseCore 1:
  399.3 123.7 all-gather.12
  565.7 108.5 all-gather.10
where the time goes:
time: 1390 us; the launch traced here: 1380 us
  waiting for transfers between devices  532 us (38%)
  starting transfers between devices  245 us (18%)
  Pallas kernels  239 us (17%)
  matrix products  201 us (14%)
  local copies, waits for them, and re-layouts  74.1 us (5%)
  other arithmetic  66.1 us (5%)
  between operations  18.8 us (1%)
    ppermute x20, waiting for transfers between devices, swap_group(): return lax.ppermute(values, DP, [(i, i ^ 1) for i in range(count)])  178 us
    pallas_call x2, Pallas kernels, gated_all(): pl.pallas_call(kernel, grid=(2 * steps,), in_specs=[near_spec, far_spec,...  113 us
    dot_general x10, matrix products, t_mm(): lax.dot_general(left, right, (((0,), (0,)), ((), ())), preferred_element_...  110 us
    ppermute x23, waiting for transfers between devices, xor_permute(): return lax.ppermute(values, ROWS, [(i, i ^ bits) for i in range(4)])  89 us
    ppermute x18, waiting for transfers between devices, swap_y(): return lax.ppermute(values, RY, [(0, 1), (1, 0)])  77.4 us
    pallas_call x10, Pallas kernels, join(): pl.pallas_call(kernel, grid_spec=pltpu.PrefetchScalarGridSpec(num_scalar_...  76.5 us
    ppermute x18, starting transfers between devices, swap_x(): return lax.ppermute(values, CX, [(0, 1), (1, 0)])  68.7 us
    ppermute x2, waiting for transfers between devices, gather_line(): pair = lax.ppermute(values, DP, [(0, 1), (1, 0), (2, 3), (3, 2)])  68.5 us
  transfers between devices with their start and end apart: 156, of which 60 were waited for; matrix products, arithmetic and copies ran while one was open for 22% of the time, Pallas kernels for 17%

commit v1 on v0

--- a/solution.py
+++ b/solution.py
@@ -325,6 +325,7 @@
     half, share = normed[0].shape[0], gate_w.shape[1]
     rows, width = 512, share // 3
     steps = half // rows
+    down_t = down_w.T
 
     def kernel(xn_ref, xf_ref, gn_ref, gf_ref, gate_ref, up_ref, down_ref, *outs):
         x_ref, g_ref, act_ref, dgate_ref, dup_ref = outs
@@ -344,14 +345,14 @@
             part = slice(tile * width, (tile + 1) * width)
             gate = mm(x_ref[...], gate_ref[:, part])
             up = mm(x_ref[...], up_ref[:, part])
-            grad_units = mm_t(g_ref[...], down_ref[part, :])
+            grad_units = mm(g_ref[...], down_ref[:, part])
             act_ref[:, part], dgate_ref[:, part], dup_ref[:, part] = gated(gate, up, grad_units)
 
     near_spec = pl.BlockSpec((rows, D), lambda i: (jnp.minimum(i, steps - 1), 0))
     far_spec = pl.BlockSpec((rows, D), lambda i: (jnp.maximum(i - steps, 0), 0))
     token_spec = pl.BlockSpec((rows, D), lambda i: (i, 0))
     out_spec = pl.BlockSpec((rows, share), lambda i: (i, 0))
-    whole = [pl.BlockSpec(weight.shape, lambda i: (0, 0)) for weight in (gate_w, up_w, down_w)]
+    whole = [pl.BlockSpec(weight.shape, lambda i: (0, 0)) for weight in (gate_w, up_w, down_t)]
     tokens = 2 * half
     return pl.pallas_call(
         kernel,
@@ -365,7 +366,7 @@
             bytes_accessed=2 * (4 * tokens * D + 3 * share * D + 3 * tokens * share),
             transcendentals=tokens * share,
         ),
-    )(*normed, *grads, gate_w, up_w, down_w)
+    )(*normed, *grads, gate_w, up_w, down_t)
 
 
 def gated(gate, up, grad_units):
@@ -412,13 +413,30 @@
         blocks = jnp.stack([values[:, i * width : (i + 1) * width] for i in range(4)])
         return lax.all_to_all(blocks, ROWS, 0, 0, tiled=True).reshape(4 * rows, width)
 
+    def pack_pair(qkv_part, out_part):
+        return jnp.concatenate([qkv_part, out_part.reshape(D // 4, -1)], axis=1)
+
+    def split_pair(packed_part):
+        return packed_part[:, : w_qkv.shape[2]], packed_part[:, w_qkv.shape[2] :].reshape(
+            w_out.shape[1], -1
+        )
+
     def fetch_attention(layer):
-        qkv_near = swap_diagonal(w_qkv[layer])
-        out_near = swap_diagonal(w_out[layer])
-        qkv_block = lax.all_gather(qkv_near, PLANE, axis=0)
-        out_block = lax.all_gather(out_near, PLANE, axis=0)
-        qkv_full = qkv_block.reshape(D, -1)
-        out_full = jnp.concatenate([out_block[i] for i in range(4)], axis=1)
+        near = swap_diagonal(pack_pair(w_qkv[layer], w_out[layer]))
+        if layer == 0:
+            half = near.shape[0] // 2
+            by_x = swap_x(near)
+            by_y = swap_y(near)
+            corner = jnp.concatenate([swap_x(by_y[:half]), swap_y(by_x[half:])], axis=0)
+            parts = [near, by_x, by_y, corner]
+            parts = [jnp.where(column == 1, parts[i ^ 1], parts[i]) for i in range(4)]
+            parts = [jnp.where(place >= 2, parts[i ^ 2], parts[i]) for i in range(4)]
+        else:
+            blocks = lax.all_gather(near, PLANE, axis=0)
+            parts = [blocks[i] for i in range(4)]
+        pairs = [split_pair(part) for part in parts]
+        qkv_full = jnp.concatenate([pair[0] for pair in pairs], axis=0)
+        out_full = jnp.concatenate([pair[1] for pair in pairs], axis=1)
         return qkv_full, out_full
 
     half_d = D // 8
@@ -505,16 +523,19 @@
         spread = arrived.reshape(4 * share, -1)[:units]
         return sum_dp(spread)
 
-    def return_qkv(grad):
-        blocks = grad.astype(bf16).reshape(4, D // 4, -1)
+    def return_attention(qkv_grad, out_grad_part):
+        rows, columns = qkv_grad.astype(bf16), out_grad_part.astype(bf16)
+        width = D // 4
+        blocks = jnp.stack(
+            [
+                pack_pair(
+                    rows[i * width : (i + 1) * width], columns[:, i * width : (i + 1) * width]
+                )
+                for i in range(4)
+            ]
+        )
         summed = lax.psum_scatter(blocks, PLANE)
-        return sum_dp(swap_diagonal(summed))
-
-    def return_out(grad):
-        rows = grad.astype(bf16)
-        blocks = jnp.stack([rows[:, i * (D // 4) : (i + 1) * (D // 4)] for i in range(4)])
-        summed = lax.psum_scatter(blocks, PLANE)
-        return sum_dp(swap_diagonal(summed))
+        return split_pair(sum_dp(swap_diagonal(summed)))
 
     def all_tokens(values, by_line):
         mine = values[: values.shape[0] // 2]
@@ -528,11 +549,10 @@
         normed, grads, activated, grad_gate, grad_up = gated_all(
             normed, grads, gate_w, up_w, down_w
         )
-        return (
-            t_mm(normed, grad_gate).astype(bf16),
-            t_mm(normed, grad_up).astype(bf16),
-            t_mm(activated, grads).astype(bf16),
-        )
+        gate_grad = t_mm(normed, grad_gate).astype(bf16)
+        up_grad = t_mm(normed, grad_up).astype(bf16)
+        down_grad = t_mm(activated, grads).astype(bf16)
+        return gate_grad, up_grad, down_grad
 
     both = tokens_whole(jnp.stack([hidden_in, out_grad]))
     resid = both[0].astype(f32)
@@ -603,19 +623,19 @@
         middle_round = grad_middle.astype(bf16)
         pair_grad = jnp.concatenate([middle_round, swap_core(middle_round)], axis=0)
         grad_heads = mm_t(pair_grad, out_full)
-        out_grad_w = return_out(t_mm(attended, pair_grad))
+        out_grad_w = t_mm(attended, pair_grad)
         grad_qkv = attention_backward(grad_heads, kept, frame)
         bias_part = jnp.sum(grad_qkv, axis=0)
         qkv_round = grad_qkv.astype(bf16)
         grad_part = mm_t(qkv_round, qkv_full)
         grad_other = swap_core(grad_part[own:].astype(bf16))
         grad_normed_attn = grad_part[:own] + grad_other.astype(f32)
-        qkv_grad_w = return_qkv(t_mm(pair_attn, qkv_round))
+        qkv_grad_w = t_mm(pair_attn, qkv_round)
         grad_first, attn_gain_part = norm_backward(
             grad_normed_attn, resid, scale_attn, attn_gain_full[layer]
         )
         grad_resid = grad_middle + grad_first
-        grads[layer] = (qkv_grad_w, out_grad_w)
+        grads[layer] = return_attention(qkv_grad_w, out_grad_w)
         small[layer] = (attn_gain_part, mlp_gain_part, bias_part)
     in_grad = features_back(grad_resid.astype(bf16)).astype(f32)
 

time: 1390 us -> 1410 us (1.014)
  local copies, waits for them, and re-layouts: 74.1 us -> 160 us
  waiting for transfers between devices: 532 us -> 476 us
    ppermute x2, starting transfers between devices: 2.05 us -> 79.3 us  [gather_line(): pair = lax.ppermute(values, DP, [(0, 1), (1, 0), (2, 3), (3, 2)])]
    ppermute x23, waiting for transfers between devices: 89 us -> 24.1 us  [xor_permute(): return lax.ppermute(values, ROWS, [(i, i ^ bits) for i in range(4)])]
    all_gather x4 -> x1, waiting for transfers between devices: 50.4 us -> 0.01 us  [fetch_attention(): blocks = lax.all_gather(near, PLANE, axis=0)]
    reshape x0 -> x24, local copies, waits for them, and re-layouts: none -> 50 us  [the longest x16 25.3 us: pack_pair(): return jnp.concatenate([qkv_part, out_part.reshape(D // 4, -1)], axis=1)]
    ppermute x18 -> x20, starting transfers between devices: 68.7 us -> 23.3 us  [swap_x(): return lax.ppermute(values, CX, [(0, 1), (1, 0)])]
    ppermute x18 -> x20, waiting for transfers between devices: 77.4 us -> 119 us  [swap_y(): return lax.ppermute(values, RY, [(0, 1), (1, 0)])]
    ppermute x2, waiting for transfers between devices: 68.5 us -> 31.2 us  [gather_line(): pair = lax.ppermute(values, DP, [(0, 1), (1, 0), (2, 3), (3, 2)])]
    ppermute x20, waiting for transfers between devices: 178 us -> 213 us  [swap_group(): return lax.ppermute(values, DP, [(i, i ^ 1) for i in range(count)])]
  transfers between devices with their start and end apart: 156 -> 145, of which waited for: 60 -> 46; matrix products, arithmetic and copies ran while one was open for 22% -> 27% of each run, Pallas kernels for 17% -> 17%
where the time goes in v1:
time: 1410 us; the launch traced here: 1400 us
  waiting for transfers between devices  476 us (34%)
  Pallas kernels  238 us (17%)
  starting transfers between devices  236 us (17%)
  matrix products  200 us (14%)
  local copies, waits for them, and re-layouts  160 us (11%)
  other arithmetic  68.2 us (5%)
  between operations  18.6 us (1%)
    ppermute x20, waiting for transfers between devices, swap_group(): return lax.ppermute(values, DP, [(i, i ^ 1) for i in range(count)])  213 us
    ppermute x20, waiting for transfers between devices, swap_y(): return lax.ppermute(values, RY, [(0, 1), (1, 0)])  119 us
    pallas_call x2, Pallas kernels, gated_all(): pl.pallas_call(kernel, grid=(2 * steps,), in_specs=[near_spec, far_spec,...  113 us
    dot_general x10, matrix products, t_mm(): lax.dot_general(left, right, (((0,), (0,)), ((), ())), preferred_element_...  109 us
    ppermute x2, starting transfers between devices, gather_line(): pair = lax.ppermute(values, DP, [(0, 1), (1, 0), (2, 3), (3, 2)])  79.3 us
    pallas_call x10, Pallas kernels, join(): pl.pallas_call(kernel, grid_spec=pltpu.PrefetchScalarGridSpec(num_scalar_...  76.2 us
    ppermute x20, waiting for transfers between devices, swap_x(): return lax.ppermute(values, CX, [(0, 1), (1, 0)])  56.1 us
    pallas_call x10, Pallas kernels, take(): pl.pallas_call(kernel, grid_spec=pltpu.PrefetchScalarGridSpec(num_scalar_...  48.8 us
  transfers between devices with their start and end apart: 145, of which 46 were waited for; matrix products, arithmetic and copies ran while one was open for 27% of the time, Pallas kernels for 17%

profile of v1, /device:TPU:0, one launch (start us, length us, event | category | flops | bytes accessed | tf_op | source)
XLA Modules:
  0.0 1397.3 jit_solution(437945440728790812)
XLA Ops:
  20.2 13.0 collective-permute-done.11
  39.8 26.3 %collective-permute-done.7 = bf16[384,1792]{1,0:T(8,128)(2,1)S(1)} collective-permute-done((bf16[384,1792]{1,0:T(8,128)(2,1)}, bf16[384,1792]{1,0:T(8,128)(2,1)S(1)}, u32[]{:S(2)}, u32[]{:S(2)}) %collective-permute-start.7) | collective-permute-done | bytes 1376288 | tf_op jit(solution)/shard_map/ppermute | solution.py:52
  70.1 13.6 collective-permute-done.8
  118.8 11.9 collective-permute-start.34
  151.9 32.5 %collective-permute-done.16 = bf16[48,1536]{1,0:T(8,128)(2,1)S(1)} collective-permute-done((bf16[48,1536]{1,0:T(8,128)(2,1)S(1)}, bf16[48,1536]{1,0:T(8,128)(2,1)S(1)}, u32[]{:S(2)}, u32[]{:S(2)}) %collective-permute-start.16) | collective-permute-done | bytes 147488 | tf_op jit(solution)/shard_map/ppermute | solution.py:52
  186.0 10.5 collective-permute-done.27.refs_5_
  201.6 7.2 shard_map.216
  208.7 11.9 collective-permute-done.20.refs_4_
  220.7 18.1 %collective-permute-done.22.refs_6_ = bf16[2,192,1152]{2,1,0:T(8,128)(2,1)} collective-permute-done((bf16[2,192,1152]{2,1,0:T(8,128)(2,1)}, bf16[2,192,1152]{2,1,0:T(8,128)(2,1)}, u32[]{:S(2)}, u32[]{:S(2)}) %collective-permute-start.22) | collective-permute-done | bytes 884768 | tf_op jit(solution)/shard_map/ppermute | solution.py:206
  238.7 8.9 shard_map.214
  303.8 11.4 reshape.268
  334.3 34.2 %collective-permute-done.49 = bf16[48,1536]{1,0:T(8,128)(2,1)S(1)} collective-permute-done((bf16[48,1536]{1,0:T(8,128)(2,1)S(1)}, bf16[48,1536]{1,0:T(8,128)(2,1)S(1)}, u32[]{:S(2)}, u32[]{:S(2)}) %collective-permute-start.49) | collective-permute-done | bytes 147488 | tf_op jit(solution)/shard_map/ppermute | solution.py:52
  401.9 6.8 shard_map.220
  408.8 28.9 %collective-permute-done.43.refs_4_ = bf16[2,192,1152]{2,1,0:T(8,128)(2,1)} collective-permute-done((bf16[2,192,1152]{2,1,0:T(8,128)(2,1)}, bf16[2,192,1152]{2,1,0:T(8,128)(2,1)}, u32[]{:S(2)}, u32[]{:S(2)}) %collective-permute-start.43) | collective-permute-done | bytes 884768 | tf_op jit(solution)/shard_map/ppermute | solution.py:206
  437.7 58.7 %collective-permute-done.45.refs_6_ = bf16[2,192,1152]{2,1,0:T(8,128)(2,1)} collective-permute-done((bf16[2,192,1152]{2,1,0:T(8,128)(2,1)}, bf16[2,192,1152]{2,1,0:T(8,128)(2,1)}, u32[]{:S(2)}, u32[]{:S(2)}) %collective-permute-start.45) | collective-permute-done | bytes 884768 | tf_op jit(solution)/shard_map/ppermute | solution.py:206
  496.4 8.8 shard_map.218
  526.9 6.2 convolution_add_fusion.1
  548.1 31.2 %collective-permute-done.106 = bf16[384,1536]{1,0:T(8,128)(2,1)} collective-permute-done((bf16[384,1536]{1,0:T(8,128)(2,1)}, bf16[384,1536]{1,0:T(8,128)(2,1)}, u32[]{:S(2)}, u32[]{:S(2)}) %collective-permute-start.106) | collective-permute-done | bytes 1179680 | tf_op jit(solution)/shard_map/ppermute | solution.py:184
  663.9 79.3 %collective-permute-start.95 = (bf16[384,1536]{1,0:T(8,128)(2,1)}, bf16[384,1536]{1,0:T(8,128)(2,1)}, u32[]{:S(2)}, u32[]{:S(2)}) collective-permute-start(bf16[384,1536]{1,0:T(8,128)(2,1)} %get-tuple-element.274), channel_id=1, source_target_pairs={{0,8},{8,0},{16,24},{24,16},{1,9},{9,1},{17,25},{25,17},{2,10},{10... | collective-permute-start | bytes 3538952 | tf_op jit(solution)/shard_map/ppermute | solution.py:184
  745.6 6.7 fusion.221
  762.6 10.0 convolution_add_fusion
  803.0 10.3 collective-permute-done.72
  880.4 7.3 collective-permute-start.83
  896.3 57.0 %shard_map.223 = (bf16[3072,1536]{1,0:T(8,128)(2,1)}, bf16[3072,1536]{1,0:T(8,128)(2,1)}, bf16[3072,1152]{1,0:T(8,128)(2,1)}, bf16[3072,1152]{1,0:T(8,128)(2,1)}, bf16[3072,1152]{1,0:T(8,128)(2,1)}) custom-call(bf16[1536,1536]{1,0:T(8,128)(2,1)} %pad_maximum_fusion.3.xn_ref, bf16[1536,1536]{1,0:T(8,128)(2,1)} %collective-permute-done.111.xf_ref, ...), custom_call_target="tpu_custom_call" | custom-call | flops 32614907904 | bytes 69599232 | tf_op jit(solution)/shard_map/pallas_call | solution.py:357
  953.2 17.9 %convolution_convert_fusion.2.refs_0_ = bf16[1536,1152]{1,0:T(8,128)(2,1)} fusion(bf16[3072,1536]{1,0:T(8,128)(2,1)} %get-tuple-element.79, bf16[3072,1152]{1,0:T(8,128)(2,1)} %get-tuple-element.88), kind=kOutput, calls=%fused_computation.4 | convolution fusion | flops 10873405440 | bytes 20054016 | tf_op jit(solution)/shard_map/dot_general | solution.py:40
  977.4 18.4 %convolution_convert_fusion.4.refs_0_ = bf16[1536,1152]{1,0:T(8,128)(2,1)} fusion(bf16[3072,1536]{1,0:T(8,128)(2,1)} %get-tuple-element.79, bf16[3072,1152]{1,0:T(8,128)(2,1)} %get-tuple-element.80), kind=kOutput, calls=%fused_computation.6 | convolution fusion | flops 10873405440 | bytes 20054016 | tf_op jit(solution)/shard_map/dot_general | solution.py:40
  1000.5 16.8 %convolution_convert_fusion.refs_0_ = bf16[1152,1536]{1,0:T(8,128)(2,1)} fusion(bf16[3072,1152]{1,0:T(8,128)(2,1)} %get-tuple-element.97, bf16[3072,1536]{1,0:T(8,128)(2,1)} %get-tuple-element.98), kind=kOutput, calls=%fused_computation.2 | convolution fusion | flops 10873405440 | bytes 20054016 | tf_op jit(solution)/shard_map/dot_general | solution.py:40
  1023.9 56.4 %shard_map.221 = (bf16[3072,1536]{1,0:T(8,128)(2,1)}, bf16[3072,1536]{1,0:T(8,128)(2,1)}, bf16[3072,1152]{1,0:T(8,128)(2,1)}, bf16[3072,1152]{1,0:T(8,128)(2,1)}, bf16[3072,1152]{1,0:T(8,128)(2,1)}) custom-call(bf16[1536,1536]{1,0:T(8,128)(2,1)} %all-gather.5.cloned.1.call-done.xn_ref, bf16[1536,1536]{1,0:T(8,128)(2,1)} %collective-permute-done.94.xf_ref, ...), custom_call_target="tpu_custom_call" | custom-call | flops 32614907904 | bytes 69599232 | tf_op jit(solution)/shard_map/pallas_call | solution.py:357
  1084.0 16.8 %convolution_convert_fusion.1.refs_0_ = bf16[1152,1536]{1,0:T(8,128)(2,1)} fusion(bf16[3072,1152]{1,0:T(8,128)(2,1)} %get-tuple-element.92, bf16[3072,1536]{1,0:T(8,128)(2,1)} %get-tuple-element.93), kind=kOutput, calls=%fused_computation.3 | convolution fusion | flops 10873405440 | bytes 20054016 | tf_op jit(solution)/shard_map/dot_general | solution.py:40
  1101.9 6.8 collective-permute-start.91
  1111.5 18.3 %convolution_convert_fusion.5.refs_0_ = bf16[1536,1152]{1,0:T(8,128)(2,1)} fusion(bf16[3072,1536]{1,0:T(8,128)(2,1)} %get-tuple-element.74, bf16[3072,1152]{1,0:T(8,128)(2,1)} %get-tuple-element.75), kind=kOutput, calls=%fused_computation.7 | convolution fusion | flops 10873405440 | bytes 20054016 | tf_op jit(solution)/shard_map/dot_general | solution.py:40
  1129.8 7.5 collective-permute-done.91
  1144.2 6.7 collective-permute-done.125.refs_3_
  1152.7 6.5 collective-permute-start.87
  1159.2 14.4 %convolution_convert_fusion.3.refs_0_ = bf16[1536,1152]{1,0:T(8,128)(2,1)} fusion(bf16[3072,1536]{1,0:T(8,128)(2,1)S(1)} %bitcast.278, bf16[3072,1152]{1,0:T(8,128)(2,1)S(1)} %bitcast.280), kind=kOutput, calls=%fused_computation.5 | convolution fusion | flops 10873405440 | bytes 20054016 | tf_op jit(solution)/shard_map/dot_general | solution.py:40
  1190.5 17.9 %collective-permute-done.87 = bf16[384,1792]{0,1:T(8,128)(2,1)} collective-permute-done((bf16[384,1792]{0,1:T(8,128)(2,1)S(1)}, bf16[384,1792]{0,1:T(8,128)(2,1)}, u32[]{:S(2)}, u32[]{:S(2)}) %collective-permute-start.87) | collective-permute-done | bytes 1376288 | tf_op jit(solution)/shard_map/ppermute | solution.py:173
  1210.1 7.9 collective-permute-done.135.refs_3_
  1231.4 8.1 collective-permute-done.104.refs_4_
  1240.3 9.7 collective-permute-done.129.refs_2_
  1266.7 36.4 %collective-permute-done.105.refs_5_ = bf16[1,192,1152]{2,1,0:T(8,128)(2,1)S(1)} collective-permute-done((bf16[1,192,1152]{2,1,0:T(8,128)(2,1)S(1)}, bf16[1,192,1152]{2,1,0:T(8,128)(2,1)S(1)}, u32[]{:S(2)}, u32[]{:S(2)}) %collective-permute-start.105) | collective-permute-done | bytes 442400 | tf_op jit(solution)/shard_map/ppermute | solution.py:206
  1303.1 9.5 collective-permute-done.130.refs_3_
  1312.6 9.5 collective-permute-done.132.refs_5_
  1324.6 7.6 shard_map.233.refs_6_
  1332.2 7.4 shard_map.225.refs_6_
  1339.6 7.4 shard_map.229.refs_6_
  1347.0 7.4 shard_map.234
  1354.4 7.4 shard_map.226
  1361.8 7.4 shard_map.230
  (901 shorter events, 537.9 us)
Async XLA Ops:
  8.0 283.8 %all-gather.9.cloned.1.call-start = ((), (), s32[]{:S(2)}) async-start(), calls=%async_computation.6 | async-start | bytes 6881280 | tf_op jit(solution)/shard_map/all_gather | solution.py:435
  118.8 80.5 %collective-permute-start.34 = (bf16[384,1792]{1,0:T(8,128)(2,1)}, bf16[384,1792]{1,0:T(8,128)(2,1)}, u32[]{:S(2)}, u32[]{:S(2)}) collective-permute-start(bf16[384,1792]{1,0:T(8,128)(2,1)} %pad_maximum_fusion.6), channel_id=1, source_target_pairs={{0,0},{1,2},{2,1},{3,3},{4,4},{5,6},{6,5},{7,7},{8,8},{9,10},{10,9... | collective-permute-start | bytes 4128776 | tf_op jit(solution)/shard_map/ppermute | solution.py:56
  138.0 59.4 %collective-permute-start.19 = (bf16[2,192,1152]{2,1,0:T(8,128)(2,1)}, bf16[2,192,1152]{2,1,0:T(8,128)(2,1)}, u32[]{:S(2)}, u32[]{:S(2)}) collective-permute-start(bf16[2,192,1152]{2,1,0:T(8,128)(2,1)} %get-tuple-element.57), channel_id=1, source_target_pairs={{0,4},{2,6},{4,0},{6,2},{1,5},{3,7},{5,1},{7,3},{8,12},{10,14},{12... | collective-permute-start | bytes 2654216 | tf_op jit(solution)/shard_map/ppermute | solution.py:201
  143.3 54.6 %collective-permute-start.21 = (bf16[2,192,1152]{2,1,0:T(8,128)(2,1)}, bf16[2,192,1152]{2,1,0:T(8,128)(2,1)}, u32[]{:S(2)}, u32[]{:S(2)}) collective-permute-start(bf16[2,192,1152]{2,1,0:T(8,128)(2,1)} %get-tuple-element.58), channel_id=1, source_target_pairs={{0,6},{2,4},{4,2},{6,0},{1,7},{3,5},{5,3},{7,1},{8,14},{10,12},{12... | collective-permute-start | bytes 2654216 | tf_op jit(solution)/shard_map/ppermute | solution.py:201
  149.0 89.8 %collective-permute-start.18 = (bf16[2,384,1152]{2,1,0:T(8,128)(2,1)}, bf16[2,384,1152]{2,1,0:T(8,128)(2,1)}, u32[]{:S(2)}, u32[]{:S(2)}) collective-permute-start(bf16[2,384,1152]{2,1,0:T(8,128)(2,1)} %get-tuple-element.56), channel_id=1, source_target_pairs={{0,2},{2,0},{1,3},{3,1},{4,6},{6,4},{5,7},{7,5},{8,10},{10,8},{9,1... | collective-permute-start | bytes 5308424 | tf_op jit(solution)/shard_map/ppermute | solution.py:44
  197.3 50.3 %collective-permute-start.17 = (bf16[384,1536]{1,0:T(8,128)(2,1)S(1)}, bf16[384,1536]{1,0:T(8,128)(2,1)}, u32[]{:S(2)}, u32[]{:S(2)}) collective-permute-start(bf16[384,1536]{1,0:T(8,128)(2,1)S(1)} %get-tuple-element.286), channel_id=1, source_target_pairs={{0,2},{2,0},{1,3},{3,1},{4,6},{6,4},{5,7},{7,5},{8,10},{10,8},{9,1... | collective-permute-start | bytes 3538952 | tf_op jit(solution)/shard_map/ppermute | solution.py:44
  199.9 396.5 %all-gather.7.cloned.1.call-start = ((), (), s32[]{:S(2)}) async-start(), calls=%async_computation.5 | async-start | bytes 5898240 | tf_op jit(solution)/shard_map/all_gather | solution.py:545
  279.1 50.5 %collective-permute-start.52 = (bf16[1,576,384]{2,1,0:T(8,128)(2,1)}, bf16[1,576,384]{2,1,0:T(8,128)(2,1)}, u32[]{:S(2)}, u32[]{:S(2)}) collective-permute-start(bf16[1,576,384]{2,1,0:T(8,128)(2,1)} %get-tuple-element.70), channel_id=1, source_target_pairs={{0,4},{2,6},{4,0},{6,2},{1,5},{3,7},{5,1},{7,3},{8,12},{10,14},{12... | collective-permute-start | bytes 1327112 | tf_op jit(solution)/shard_map/ppermute | solution.py:201
  280.8 51.8 %collective-permute-start.54 = (bf16[1,576,384]{2,1,0:T(8,128)(2,1)}, bf16[1,576,384]{2,1,0:T(8,128)(2,1)}, u32[]{:S(2)}, u32[]{:S(2)}) collective-permute-start(bf16[1,576,384]{2,1,0:T(8,128)(2,1)} %get-tuple-element.71), channel_id=1, source_target_pairs={{0,6},{2,4},{4,2},{6,0},{1,7},{3,5},{5,3},{7,1},{8,14},{10,12},{12... | collective-permute-start | bytes 1327112 | tf_op jit(solution)/shard_map/ppermute | solution.py:201
  324.1 64.1 %collective-permute-start.42 = (bf16[2,192,1152]{2,1,0:T(8,128)(2,1)}, bf16[2,192,1152]{2,1,0:T(8,128)(2,1)}, u32[]{:S(2)}, u32[]{:S(2)}) collective-permute-start(bf16[2,192,1152]{2,1,0:T(8,128)(2,1)} %get-tuple-element.65), channel_id=1, source_target_pairs={{0,4},{2,6},{4,0},{6,2},{1,5},{3,7},{5,1},{7,3},{8,12},{10,14},{12... | collective-permute-start | bytes 2654216 | tf_op jit(solution)/shard_map/ppermute | solution.py:201
  325.6 64.4 %collective-permute-start.44 = (bf16[2,192,1152]{2,1,0:T(8,128)(2,1)}, bf16[2,192,1152]{2,1,0:T(8,128)(2,1)}, u32[]{:S(2)}, u32[]{:S(2)}) collective-permute-start(bf16[2,192,1152]{2,1,0:T(8,128)(2,1)} %get-tuple-element.66), channel_id=1, source_target_pairs={{0,6},{2,4},{4,2},{6,0},{1,7},{3,5},{5,3},{7,1},{8,14},{10,12},{12... | collective-permute-start | bytes 2654216 | tf_op jit(solution)/shard_map/ppermute | solution.py:201
  370.6 125.8 %collective-permute-start.41 = (bf16[2,384,1152]{2,1,0:T(8,128)(2,1)}, bf16[2,384,1152]{2,1,0:T(8,128)(2,1)}, u32[]{:S(2)}, u32[]{:S(2)}) collective-permute-start(bf16[2,384,1152]{2,1,0:T(8,128)(2,1)} %get-tuple-element.64), channel_id=1, source_target_pairs={{0,2},{2,0},{1,3},{3,1},{4,6},{6,4},{5,7},{7,5},{8,10},{10,8},{9,1... | collective-permute-start | bytes 5308424 | tf_op jit(solution)/shard_map/ppermute | solution.py:44
  381.3 123.9 %collective-permute-start.50 = (bf16[384,1536]{1,0:T(8,128)(2,1)}, bf16[384,1536]{1,0:T(8,128)(2,1)}, u32[]{:S(2)}, u32[]{:S(2)}) collective-permute-start(bf16[384,1536]{1,0:T(8,128)(2,1)} %get-tuple-element.278), channel_id=1, source_target_pairs={{0,2},{2,0},{1,3},{3,1},{4,6},{6,4},{5,7},{7,5},{8,10},{10,8},{9,1... | collective-permute-start | bytes 3538952 | tf_op jit(solution)/shard_map/ppermute | solution.py:44
  396.0 100.4 %collective-permute-start.45 = (bf16[2,192,1152]{2,1,0:T(8,128)(2,1)}, bf16[2,192,1152]{2,1,0:T(8,128)(2,1)}, u32[]{:S(2)}, u32[]{:S(2)}) collective-permute-start(bf16[2,192,1152]{2,1,0:T(8,128)(2,1)} %collective-permute-done.44.refs_5_), channel_id=1, source_target_pairs={{0,8},{8,0},{16,24},{24,16},{1,9},{9,1},{17,25},{25,17},{2,10},{10... | collective-permute-start | bytes 2654216 | tf_op jit(solution)/shard_map/ppermute | solution.py:206
  401.8 111.9 %collective-permute-start.40 = (bf16[384,1536]{1,0:T(8,128)(2,1)}, bf16[384,1536]{1,0:T(8,128)(2,1)}, u32[]{:S(2)}, u32[]{:S(2)}) collective-permute-start(bf16[384,1536]{1,0:T(8,128)(2,1)} %get-tuple-element.282), channel_id=1, source_target_pairs={{0,2},{2,0},{1,3},{3,1},{4,6},{6,4},{5,7},{7,5},{8,10},{10,8},{9,1... | collective-permute-start | bytes 3538952 | tf_op jit(solution)/shard_map/ppermute | solution.py:44
  401.9 478.1 %all-gather.5.cloned.1.call-start = ((), (), s32[]{:S(2)}) async-start(), calls=%async_computation.4 | async-start | bytes 5898240 | tf_op jit(solution)/shard_map/all_gather | solution.py:545
  546.4 535.6 %reduce-scatter.9.cloned.1.call-start = ((), (), s32[]{:S(2)}) async-start(), calls=%async_computation.8 | async-start | bytes 6881280
  546.4 50.4 %collective-permute-start.109 = (bf16[384,1536]{1,0:T(8,128)(2,1)}, bf16[384,1536]{1,0:T(8,128)(2,1)}, u32[]{:S(2)}, u32[]{:S(2)}) collective-permute-start(bf16[384,1536]{1,0:T(8,128)(2,1)} %get-tuple-element.282), channel_id=1, source_target_pairs={{8,16},{16,8},{9,17},{17,9},{10,18},{18,10},{11,19},{19,11},{12,20... | collective-permute-start | bytes 3538952 | tf_op jit(solution)/shard_map/ppermute | solution.py:185
  596.4 299.9 %collective-permute-start.112 = (bf16[1536,1536]{1,0:T(8,128)(2,1)}, bf16[1536,1536]{1,0:T(8,128)(2,1)}, u32[]{:S(2)}, u32[]{:S(2)}) collective-permute-start(bf16[1536,1536]{1,0:T(8,128)(2,1)} %all-gather.7.cloned.1.call-done.gn_ref), channel_id=1, source_target_pairs={{0,2},{2,0},{1,3},{3,1},{4,6},{6,4},{5,7},{7,5},{8,10},{10,8},{9,1... | collective-permute-start | bytes 14155784 | tf_op jit(solution)/shard_map/ppermute | solution.py:44
  596.9 175.9 %collective-permute-start.110 = (bf16[384,1536]{1,0:T(8,128)(2,1)}, bf16[384,1536]{1,0:T(8,128)(2,1)}, u32[]{:S(2)}, u32[]{:S(2)}) collective-permute-start(bf16[384,1536]{1,0:T(8,128)(2,1)} %collective-permute-done.109), channel_id=1, source_target_pairs={{8,0},{16,24},{9,1},{17,25},{10,2},{18,26},{11,3},{19,27},{12,4},{... | collective-permute-start | bytes 3538952 | tf_op jit(solution)/shard_map/ppermute | solution.py:186
  598.2 174.7 %collective-permute-start.108 = (bf16[384,1536]{1,0:T(8,128)(2,1)}, bf16[384,1536]{1,0:T(8,128)(2,1)}, u32[]{:S(2)}, u32[]{:S(2)}) collective-permute-start(bf16[384,1536]{1,0:T(8,128)(2,1)} %collective-permute-done.107), channel_id=1, source_target_pairs={{8,0},{16,24},{9,1},{17,25},{10,2},{18,26},{11,3},{19,27},{12,4},{... | collective-permute-start | bytes 3538952 | tf_op jit(solution)/shard_map/ppermute | solution.py:188
  655.7 87.5 %collective-permute-start.67 = (bf16[384,1536]{1,0:T(8,128)(2,1)}, bf16[384,1536]{1,0:T(8,128)(2,1)}, u32[]{:S(2)}, u32[]{:S(2)}) collective-permute-start(bf16[384,1536]{1,0:T(8,128)(2,1)} %get-tuple-element.274), channel_id=1, source_target_pairs={{0,2},{2,0},{1,3},{3,1},{4,6},{6,4},{5,7},{7,5},{8,10},{10,8},{9,1... | collective-permute-start | bytes 3538952 | tf_op jit(solution)/shard_map/ppermute | solution.py:44
  663.9 115.3 %collective-permute-start.95 = (bf16[384,1536]{1,0:T(8,128)(2,1)}, bf16[384,1536]{1,0:T(8,128)(2,1)}, u32[]{:S(2)}, u32[]{:S(2)}) collective-permute-start(bf16[384,1536]{1,0:T(8,128)(2,1)} %get-tuple-element.274), channel_id=1, source_target_pairs={{0,8},{8,0},{16,24},{24,16},{1,9},{9,1},{17,25},{25,17},{2,10},{10... | collective-permute-start | bytes 3538952 | tf_op jit(solution)/shard_map/ppermute | solution.py:184
  777.5 52.9 %collective-permute-start.98 = (bf16[384,1536]{1,0:T(8,128)(2,1)}, bf16[384,1536]{1,0:T(8,128)(2,1)}, u32[]{:S(2)}, u32[]{:S(2)}) collective-permute-start(bf16[384,1536]{1,0:T(8,128)(2,1)} %get-tuple-element.274), channel_id=1, source_target_pairs={{8,16},{16,8},{9,17},{17,9},{10,18},{18,10},{11,19},{19,11},{12,20... | collective-permute-start | bytes 3538952 | tf_op jit(solution)/shard_map/ppermute | solution.py:185
  779.2 52.5 %collective-permute-start.96 = (bf16[384,1536]{1,0:T(8,128)(2,1)}, bf16[384,1536]{1,0:T(8,128)(2,1)}, u32[]{:S(2)}, u32[]{:S(2)}) collective-permute-start(bf16[384,1536]{1,0:T(8,128)(2,1)} %collective-permute-done.95), channel_id=1, source_target_pairs={{8,16},{16,8},{9,17},{17,9},{10,18},{18,10},{11,19},{19,11},{12,20... | collective-permute-start | bytes 3538952 | tf_op jit(solution)/shard_map/ppermute | solution.py:187
  819.1 289.6 %reduce-scatter.7.cloned.1.call-start = ((), (), s32[]{:S(2)}) async-start(), calls=%async_computation.7 | async-start | bytes 6881280
  829.9 66.3 %collective-permute-start.111 = (bf16[1536,1536]{1,0:T(8,128)(2,1)}, bf16[1536,1536]{1,0:T(8,128)(2,1)}, u32[]{:S(2)}, u32[]{:S(2)}) collective-permute-start(bf16[1536,1536]{1,0:T(8,128)(2,1)} %pad_maximum_fusion.3.xn_ref), channel_id=1, source_target_pairs={{0,2},{2,0},{1,3},{3,1},{4,6},{6,4},{5,7},{7,5},{8,10},{10,8},{9,1... | collective-permute-start | bytes 14155784 | tf_op jit(solution)/shard_map/ppermute | solution.py:44
  830.4 50.0 %collective-permute-start.99 = (bf16[384,1536]{1,0:T(8,128)(2,1)}, bf16[384,1536]{1,0:T(8,128)(2,1)}, u32[]{:S(2)}, u32[]{:S(2)}) collective-permute-start(bf16[384,1536]{1,0:T(8,128)(2,1)} %collective-permute-done.98), channel_id=1, source_target_pairs={{8,0},{16,24},{9,1},{17,25},{10,2},{18,26},{11,3},{19,27},{12,4},{... | collective-permute-start | bytes 3538952 | tf_op jit(solution)/shard_map/ppermute | solution.py:186
  831.7 56.0 %collective-permute-start.97 = (bf16[384,1536]{1,0:T(8,128)(2,1)}, bf16[384,1536]{1,0:T(8,128)(2,1)}, u32[]{:S(2)}, u32[]{:S(2)}) collective-permute-start(bf16[384,1536]{1,0:T(8,128)(2,1)} %collective-permute-done.96), channel_id=1, source_target_pairs={{8,0},{16,24},{9,1},{17,25},{10,2},{18,26},{11,3},{19,27},{12,4},{... | collective-permute-start | bytes 3538952 | tf_op jit(solution)/shard_map/ppermute | solution.py:188
  880.0 142.0 %collective-permute-start.94 = (bf16[1536,1536]{1,0:T(8,128)(2,1)}, bf16[1536,1536]{1,0:T(8,128)(2,1)}, u32[]{:S(2)}, u32[]{:S(2)}) collective-permute-start(bf16[1536,1536]{1,0:T(8,128)(2,1)} %all-gather.5.cloned.1.call-done.xn_ref), channel_id=1, source_target_pairs={{0,2},{2,0},{1,3},{3,1},{4,6},{6,4},{5,7},{7,5},{8,10},{10,8},{9,1... | collective-permute-start | bytes 14155784 | tf_op jit(solution)/shard_map/ppermute | solution.py:44
  894.0 129.3 %collective-permute-start.100 = (bf16[1536,1536]{1,0:T(8,128)(2,1)}, bf16[1536,1536]{1,0:T(8,128)(2,1)}, u32[]{:S(2)}, u32[]{:S(2)}) collective-permute-start(bf16[1536,1536]{1,0:T(8,128)(2,1)} %pad_maximum_fusion.2.gn_ref), channel_id=1, source_target_pairs={{0,2},{2,0},{1,3},{3,1},{4,6},{6,4},{5,7},{7,5},{8,10},{10,8},{9,1... | collective-permute-start | bytes 14155784 | tf_op jit(solution)/shard_map/ppermute | solution.py:44
  894.1 186.3 %collective-permute-start.85 = (f32[2,5120]{1,0:T(2,128)S(1)}, f32[2,5120]{1,0:T(2,128)S(1)}, u32[]{:S(2)}, u32[]{:S(2)}) collective-permute-start(f32[2,5120]{1,0:T(2,128)S(1)} %add.365), channel_id=1, source_target_pairs={{8,0},{16,24},{9,1},{17,25},{10,2},{18,26},{11,3},{19,27},{12,4},{... | collective-permute-start | bytes 122888 | tf_op jit(solution)/shard_map/ppermute | solution.py:177
  975.8 105.7 %collective-permute-start.124 = (bf16[1,192,1152]{2,1,0:T(8,128)(2,1)}, bf16[1,192,1152]{2,1,0:T(8,128)(2,1)S(1)}, u32[]{:S(2)}, u32[]{:S(2)}) collective-permute-start(bf16[1,192,1152]{2,1,0:T(8,128)(2,1)} %get-tuple-element.90), channel_id=1, source_target_pairs={{0,4},{2,6},{4,0},{6,2},{1,5},{3,7},{5,1},{7,3},{8,12},{10,14},{12... | collective-permute-start | bytes 1327112 | tf_op jit(solution)/shard_map/ppermute | solution.py:201
  976.9 105.1 %collective-permute-start.126 = (bf16[1,192,1152]{2,1,0:T(8,128)(2,1)}, bf16[1,192,1152]{2,1,0:T(8,128)(2,1)}, u32[]{:S(2)}, u32[]{:S(2)}) collective-permute-start(bf16[1,192,1152]{2,1,0:T(8,128)(2,1)} %get-tuple-element.91), channel_id=1, source_target_pairs={{0,6},{2,4},{4,2},{6,0},{1,7},{3,5},{5,3},{7,1},{8,14},{10,12},{12... | collective-permute-start | bytes 1327112 | tf_op jit(solution)/shard_map/ppermute | solution.py:201
  1021.9 78.9 %collective-permute-start.114 = (bf16[1,192,1152]{2,1,0:T(8,128)(2,1)}, bf16[1,192,1152]{2,1,0:T(8,128)(2,1)}, u32[]{:S(2)}, u32[]{:S(2)}) collective-permute-start(bf16[1,192,1152]{2,1,0:T(8,128)(2,1)} %get-tuple-element.82), channel_id=1, source_target_pairs={{0,4},{2,6},{4,0},{6,2},{1,5},{3,7},{5,1},{7,3},{8,12},{10,14},{12... | collective-permute-start | bytes 1327112 | tf_op jit(solution)/shard_map/ppermute | solution.py:201
  1023.3 78.0 %collective-permute-start.116 = (bf16[1,192,1152]{2,1,0:T(8,128)(2,1)}, bf16[1,192,1152]{2,1,0:T(8,128)(2,1)}, u32[]{:S(2)}, u32[]{:S(2)}) collective-permute-start(bf16[1,192,1152]{2,1,0:T(8,128)(2,1)} %get-tuple-element.83), channel_id=1, source_target_pairs={{0,6},{2,4},{4,2},{6,0},{1,7},{3,5},{5,3},{7,1},{8,14},{10,12},{12... | collective-permute-start | bytes 1327112 | tf_op jit(solution)/shard_map/ppermute | solution.py:201
  1142.0 45.6 %collective-permute-start.127 = (bf16[1,192,1152]{2,1,0:T(8,128)(2,1)}, bf16[1,192,1152]{2,1,0:T(8,128)(2,1)}, u32[]{:S(2)}, u32[]{:S(2)}) collective-permute-start(bf16[1,192,1152]{2,1,0:T(8,128)(2,1)} %collective-permute-done.126.refs_4_), channel_id=1, source_target_pairs={{0,8},{8,0},{16,24},{24,16},{1,9},{9,1},{17,25},{25,17},{2,10},{10... | collective-permute-start | bytes 1327112 | tf_op jit(solution)/shard_map/ppermute | solution.py:206
  1142.1 45.6 %collective-permute-start.115 = (bf16[1,192,1152]{2,1,0:T(8,128)(2,1)}, bf16[1,192,1152]{2,1,0:T(8,128)(2,1)}, u32[]{:S(2)}, u32[]{:S(2)}) collective-permute-start(bf16[1,192,1152]{2,1,0:T(8,128)(2,1)} %collective-permute-done.114.refs_2_), channel_id=1, source_target_pairs={{0,8},{8,0},{16,24},{24,16},{1,9},{9,1},{17,25},{25,17},{2,10},{10... | collective-permute-start | bytes 1327112 | tf_op jit(solution)/shard_map/ppermute | solution.py:206
  1144.1 45.6 %collective-permute-start.117 = (bf16[1,192,1152]{2,1,0:T(8,128)(2,1)}, bf16[1,192,1152]{2,1,0:T(8,128)(2,1)}, u32[]{:S(2)}, u32[]{:S(2)}) collective-permute-start(bf16[1,192,1152]{2,1,0:T(8,128)(2,1)} %collective-permute-done.116.refs_4_), channel_id=1, source_target_pairs={{0,8},{8,0},{16,24},{24,16},{1,9},{9,1},{17,25},{25,17},{2,10},{10... | collective-permute-start | bytes 1327112 | tf_op jit(solution)/shard_map/ppermute | solution.py:206
  1150.9 77.9 %collective-permute-start.92 = (bf16[384,1792]{0,1:T(8,128)(2,1)S(1)}, bf16[384,1792]{0,1:T(8,128)(2,1)}, u32[]{:S(2)}, u32[]{:S(2)}) collective-permute-start(bf16[384,1792]{0,1:T(8,128)(2,1)S(1)} %add_convert_fusion.1), channel_id=1, source_target_pairs={{8,16},{16,8},{9,17},{17,9},{10,18},{18,10},{11,19},{19,11},{12,20... | collective-permute-start | bytes 4128776 | tf_op jit(solution)/shard_map/ppermute | solution.py:175
  1152.7 55.7 %collective-permute-start.87 = (bf16[384,1792]{0,1:T(8,128)(2,1)S(1)}, bf16[384,1792]{0,1:T(8,128)(2,1)}, u32[]{:S(2)}, u32[]{:S(2)}) collective-permute-start(bf16[384,1792]{0,1:T(8,128)(2,1)S(1)} %collective-permute-done.86), channel_id=1, source_target_pairs={{0,8},{24,16},{1,9},{25,17},{2,10},{26,18},{3,11},{27,19},{4,12},{... | collective-permute-start | bytes 4128776 | tf_op jit(solution)/shard_map/ppermute | solution.py:173
  1258.5 110.7 %collective-permute-start.93 = (bf16[384,1792]{0,1:T(8,128)(2,1)S(1)}, bf16[384,1792]{0,1:T(8,128)(2,1)}, u32[]{:S(2)}, u32[]{:S(2)}) collective-permute-start(bf16[384,1792]{0,1:T(8,128)(2,1)S(1)} %add_convert_fusion), channel_id=1, source_target_pairs={{8,0},{16,24},{9,1},{17,25},{10,2},{18,26},{11,3},{19,27},{12,4},{... | collective-permute-start | bytes 4128776 | tf_op jit(solution)/shard_map/ppermute | solution.py:177
  1259.9 101.9 %collective-permute-start.118 = (bf16[1,384,1152]{2,1,0:T(8,128)(2,1)}, bf16[1,384,1152]{2,1,0:T(8,128)(2,1)}, u32[]{:S(2)}, u32[]{:S(2)}) collective-permute-start(bf16[1,384,1152]{2,1,0:T(8,128)(2,1)} %get-tuple-element.85), channel_id=1, source_target_pairs={{0,2},{2,0},{1,3},{3,1},{4,6},{6,4},{5,7},{7,5},{8,10},{10,8},{9,1... | collective-permute-start | bytes 2654216 | tf_op jit(solution)/shard_map/ppermute | solution.py:44
  1264.2 48.4 %collective-permute-start.130 = (bf16[1,576,384]{2,1,0:T(8,128)(2,1)S(1)}, bf16[1,576,384]{2,1,0:T(8,128)(2,1)S(1)}, u32[]{:S(2)}, u32[]{:S(2)}) collective-permute-start(bf16[1,576,384]{2,1,0:T(8,128)(2,1)S(1)} %collective-permute-done.129.refs_2_), channel_id=1, source_target_pairs={{0,8},{8,0},{16,24},{24,16},{1,9},{9,1},{17,25},{25,17},{2,10},{10... | collective-permute-start | bytes 1327112 | tf_op jit(solution)/shard_map/ppermute | solution.py:206
  1265.0 57.0 %collective-permute-start.132 = (bf16[1,576,384]{2,1,0:T(8,128)(2,1)S(1)}, bf16[1,576,384]{2,1,0:T(8,128)(2,1)S(1)}, u32[]{:S(2)}, u32[]{:S(2)}) collective-permute-start(bf16[1,576,384]{2,1,0:T(8,128)(2,1)S(1)} %collective-permute-done.131.refs_4_), channel_id=1, source_target_pairs={{0,8},{8,0},{16,24},{24,16},{1,9},{9,1},{17,25},{25,17},{2,10},{10... | collective-permute-start | bytes 1327112 | tf_op jit(solution)/shard_map/ppermute | solution.py:206
  1303.1 58.7 %collective-permute-start.120 = (bf16[1,192,1152]{2,1,0:T(8,128)(2,1)}, bf16[1,192,1152]{2,1,0:T(8,128)(2,1)}, u32[]{:S(2)}, u32[]{:S(2)}) collective-permute-start(bf16[1,192,1152]{2,1,0:T(8,128)(2,1)} %collective-permute-done.119.refs_2_), channel_id=1, source_target_pairs={{0,8},{8,0},{16,24},{24,16},{1,9},{9,1},{17,25},{25,17},{2,10},{10... | collective-permute-start | bytes 1327112 | tf_op jit(solution)/shard_map/ppermute | solution.py:206
  1312.6 49.2 %collective-permute-start.122 = (bf16[1,192,1152]{2,1,0:T(8,128)(2,1)}, bf16[1,192,1152]{2,1,0:T(8,128)(2,1)}, u32[]{:S(2)}, u32[]{:S(2)}) collective-permute-start(bf16[1,192,1152]{2,1,0:T(8,128)(2,1)} %collective-permute-done.121.refs_4_), channel_id=1, source_target_pairs={{0,8},{8,0},{16,24},{24,16},{1,9},{9,1},{17,25},{25,17},{2,10},{10... | collective-permute-start | bytes 1327112 | tf_op jit(solution)/shard_map/ppermute | solution.py:206
  1322.0 56.0 %collective-permute-start.89 = (bf16[384,1792]{0,1:T(8,128)(2,1)S(1)}, bf16[384,1792]{0,1:T(8,128)(2,1)}, u32[]{:S(2)}, u32[]{:S(2)}) collective-permute-start(bf16[384,1792]{0,1:T(8,128)(2,1)S(1)} %add_convert_fusion.2), channel_id=1, source_target_pairs={{8,0},{16,24},{9,1},{17,25},{10,2},{18,26},{11,3},{19,27},{12,4},{... | collective-permute-start | bytes 4128776 | tf_op jit(solution)/shard_map/ppermute | solution.py:177
  (275 other events, 4441.1 us)
Sparse Core Ops, SparseCore 0:
  200.0 62.7 all-gather.8
  662.3 151.8 reduce-scatter.8
  866.6 68.8 reduce-scatter.6
Sparse Core Ops, SparseCore 1:
  402.0 109.0 all-gather.6
  546.4 129.5 all-gather.4
